TPU v7x, 32 devices: a whole 2x2x4 slice. The times are simulated.
32 devices in a mesh: seq: 16 (over z, x, core), head: 2 (over y).
Axes of the slice: x: 2, y: 2, z: 4, core: 2. Of those that a mesh axis runs over, the one named last changes fastest.
Arguments:
- packed_inputs_slab: bfloat16 [2048, 4096], P(('seq', 'head')), may hold values from -6 to 6
- lagged_blend_coefs: float32 [5, 4096], replicated, may hold values from 0 to 1
- acceptor_projector: bfloat16 [4096, 4096], P('seq', 'head'), may hold values from -0.09375 to 0.09375
- address_projector: bfloat16 [4096, 4096], P('seq', 'head'), may hold values from -0.09375 to 0.09375
- payload_projector: bfloat16 [4096, 4096], P('seq', 'head'), may hold values from -0.09375 to 0.09375
- fading_offset_entry: float32 [4096], P('head'), may hold values from -12 to -2
- fading_left_matrix: bfloat16 [4096, 128], replicated, may hold values from -0.09375 to 0.09375
- fading_right_matrix: bfloat16 [128, 4096], P(None, 'head'), may hold values from -0.5 to 0.5
- learning_rate_offset: float32 [4096], P('head'), may hold values from -4 to 4
- learning_left_matrix: bfloat16 [4096, 128], replicated, may hold values from -0.09375 to 0.09375
- learning_right_matrix: bfloat16 [128, 4096], P(None, 'head'), may hold values from -0.5 to 0.5
- address_before_unitize: float32 [4096], P('head'), may hold values from 0.5 to 1.5
- address_learning_strength: float32 [4096], P('head'), may hold values from 0.5 to 1.5
- extra_reward_coefs: float32 [4096], P('head'), may hold values from -0.6 to 0.6
- cluster_normalize_multiplier: float32 [4096], P('head'), may hold values from 0.5 to 1.5
- paper_spans_sizes: int32 [4], replicated, may hold values from 1 to 16, 32 in all
Outputs:
- time_mixed: bfloat16 [2048, 4096], P('seq', 'head')
Inputs may be any that keep to these rules, and one draw needn't show every extreme that they name: `paper_spans_sizes`: the lengths sum to 32 and the longest is exactly 16.
All inputs are finite; a program needn't handle non-finite values.
Results may differ from a plain program's by a relative error of at most 0.0077.
Values may be sent and summed in bfloat16 or wider, within the bound.
A program may use at most 128 MiB of HBM per device.

v0:
```python
import jax
import jax.numpy as jnp
from jax import lax
from jax.sharding import PartitionSpec as P

LANE_FEATURES = 64
SPAN = 64


exact_precision = lax.Precision.HIGHEST
norm_eps = 1e-05
decay_limit = 0.606531


def passed_along(block, axis, distance):
    devices = range(lax.axis_size(axis))
    route = [(i - distance, i) for i in devices if i - distance in devices]
    return lax.ppermute(block, axis, route)


def product(left, right):
    return jnp.matmul(left, right, precision=exact_precision)


def flipped(matrix):
    return jnp.swapaxes(matrix, -1, -2)


def mixed_inputs(packed_inputs_slab, earlier, lagged_blend_coefs):
    current = packed_inputs_slab.astype(jnp.float32)
    change = earlier.astype(jnp.float32) - current
    return [
        (current + change * lagged_blend_coefs[member]).astype(jnp.bfloat16) for member in range(5)
    ]


def prepare(
    acceptor_lines,
    keyed,
    payload_entries,
    x_decay,
    x_icl,
    fading_offset_entry,
    fading_left_matrix,
    fading_right_matrix,
    learning_rate_offset,
    learning_left_matrix,
    learning_right_matrix,
    address_before_unitize,
    address_learning_strength,
):
    decay_low = jnp.tanh(
        jnp.dot(x_decay, fading_left_matrix, preferred_element_type=jnp.float32)
    ).astype(jnp.bfloat16)
    log_decay = -decay_limit * jax.nn.sigmoid(
        fading_offset_entry
        + jnp.dot(decay_low, fading_right_matrix, preferred_element_type=jnp.float32)
    )
    icl_low = jnp.dot(x_icl, learning_left_matrix, preferred_element_type=jnp.float32).astype(
        jnp.bfloat16
    )
    icl = jax.nn.sigmoid(
        learning_rate_offset
        + jnp.dot(icl_low, learning_right_matrix, preferred_element_type=jnp.float32)
    )
    row_count = acceptor_lines.shape[0]
    attention_lane_count = acceptor_lines.shape[1] // LANE_FEATURES
    head_shape = (row_count, attention_lane_count, LANE_FEATURES)
    scaled = (keyed * address_before_unitize).reshape(head_shape)
    unit_key = scaled / jnp.sqrt(jnp.sum(scaled * scaled, axis=-1, keepdims=True) + norm_eps)
    icl_heads = icl.reshape(head_shape)
    adjusted_address = keyed.reshape(head_shape) * (
        1.0
        + (icl_heads - 1.0) * address_learning_strength.reshape(attention_lane_count, LANE_FEATURES)
    )
    return (
        acceptor_lines.reshape(head_shape),
        adjusted_address,
        payload_entries.reshape(head_shape),
        log_decay.reshape(head_shape),
        -unit_key,
        unit_key * icl_heads,
    )


def ending_result(
    result_lines,
    acceptor_lines,
    adjusted_address,
    payload_entries,
    extra_reward_coefs,
    cluster_normalize_multiplier,
):
    attention_lane_count = result_lines.shape[1]
    average = jnp.mean(result_lines, axis=-1, keepdims=True)
    centered = result_lines - average
    spread = jnp.mean(centered * centered, axis=-1, keepdims=True)
    unitized_result = (
        centered
        / jnp.sqrt(spread + norm_eps)
        * cluster_normalize_multiplier.reshape(attention_lane_count, LANE_FEATURES)
    )
    present_reward = (
        jnp.sum(
            acceptor_lines
            * adjusted_address
            * extra_reward_coefs.reshape(attention_lane_count, LANE_FEATURES),
            axis=-1,
            keepdims=True,
        )
        * payload_entries
    )
    return (
        (unitized_result + present_reward).reshape(result_lines.shape[0], -1).astype(jnp.bfloat16)
    )


def span_terms(log_decay, acceptor_lines, keyed, alpha, beta):
    length = log_decay.shape[-2]
    log_sums = jnp.cumsum(log_decay, axis=-2)
    decay_in = jnp.exp(log_sums)
    decay_before = jnp.exp(log_sums - log_decay)
    inverse = jnp.exp(-log_sums)
    decay_out = jnp.exp(log_sums[..., -1:, :] - log_sums)
    alpha_dec = alpha * decay_before
    recept_dec = acceptor_lines * decay_in
    beta_inv = beta * inverse
    key_inv = keyed * inverse
    row_index = lax.broadcasted_iota(jnp.int32, (length, length), 0)
    col_index = lax.broadcasted_iota(jnp.int32, (length, length), 1)
    strict = row_index > col_index
    on_or_below = row_index >= col_index
    solve_matrix = jnp.eye(length, dtype=jnp.float32) - jnp.where(
        strict, product(alpha_dec, flipped(beta_inv)), 0.0
    )
    key_read = jnp.where(strict, product(alpha_dec, flipped(key_inv)), 0.0)
    out_beta = jnp.where(on_or_below, product(recept_dec, flipped(beta_inv)), 0.0)
    out_key = jnp.where(on_or_below, product(recept_dec, flipped(key_inv)), 0.0)
    return (
        solve_matrix,
        key_read,
        out_beta,
        out_key,
        alpha_dec,
        recept_dec,
        decay_in[..., -1, :],
        decay_out,
    )


def per_device(
    packed_inputs_slab,
    lagged_blend_coefs,
    acceptor_projector,
    address_projector,
    payload_projector,
    fading_offset_entry,
    fading_left_matrix,
    fading_right_matrix,
    learning_rate_offset,
    learning_left_matrix,
    learning_right_matrix,
    address_before_unitize,
    address_learning_strength,
    extra_reward_coefs,
    cluster_normalize_multiplier,
    paper_spans_sizes,
):
    gathered = lax.all_gather(packed_inputs_slab, "head", axis=0, tiled=True)
    row_count = gathered.shape[0]
    block_count = row_count // SPAN
    doc_starts = jnp.cumsum(paper_spans_sizes) - paper_spans_sizes
    span_ids = lax.axis_index("seq") * block_count + jnp.arange(block_count, dtype=jnp.int32)
    resets = jnp.any(doc_starts[None, :] == span_ids[:, None], axis=1)
    edge_token = passed_along(gathered[-1:], "seq", 1)
    earlier = jnp.concatenate([edge_token, gathered[:-1]], axis=0)
    row_start = jnp.logical_and(jnp.arange(row_count) % SPAN == 0, jnp.repeat(resets, SPAN))
    earlier = jnp.where(row_start[:, None], jnp.zeros_like(earlier), earlier)
    x_recept, x_decay, x_key, x_value, x_icl = mixed_inputs(gathered, earlier, lagged_blend_coefs)
    whole_recept = lax.all_gather(acceptor_projector, "seq", axis=0, tiled=True)
    whole_key = lax.all_gather(address_projector, "seq", axis=0, tiled=True)
    whole_value = lax.all_gather(payload_projector, "seq", axis=0, tiled=True)
    acceptor_lines = jnp.dot(x_recept, whole_recept, preferred_element_type=jnp.float32)
    keyed = jnp.dot(x_key, whole_key, preferred_element_type=jnp.float32)
    payload_entries = jnp.dot(x_value, whole_value, preferred_element_type=jnp.float32)
    acceptor_lines, adjusted_address, payload_entries, log_decay, alpha, beta = prepare(
        acceptor_lines,
        keyed,
        payload_entries,
        x_decay,
        x_icl,
        fading_offset_entry,
        fading_left_matrix,
        fading_right_matrix,
        learning_rate_offset,
        learning_left_matrix,
        learning_right_matrix,
        address_before_unitize,
        address_learning_strength,
    )
    attention_lane_count = acceptor_lines.shape[1]

    def blocks(array):
        return jnp.swapaxes(
            array.reshape(block_count, SPAN, attention_lane_count, LANE_FEATURES), 1, 2
        )

    recept_b, key_b, value_b, decay_b, alpha_b, beta_b = [
        blocks(array)
        for array in (acceptor_lines, adjusted_address, payload_entries, log_decay, alpha, beta)
    ]
    solve_matrix, key_read, out_beta, out_key, alpha_dec, recept_dec, decay_last, decay_out = (
        span_terms(decay_b, recept_b, key_b, alpha_b, beta_b)
    )
    right_side = jnp.concatenate([alpha_dec, product(key_read, value_b)], axis=-1)
    solved = jax.scipy.linalg.solve_triangular(
        solve_matrix, right_side, lower=True, unit_diagonal=True
    )
    linear_reads = solved[..., :LANE_FEATURES]
    offset_reads = solved[..., LANE_FEATURES:]
    queries = recept_dec + product(out_beta, linear_reads)
    output_base = product(out_beta, offset_reads) + product(out_key, value_b)
    beta_out = beta_b * decay_out
    identity = jnp.eye(LANE_FEATURES, dtype=jnp.float32)
    step_map = identity * decay_last[..., None, :] + product(flipped(linear_reads), beta_out)
    step_add = product(flipped(offset_reads), beta_out) + product(
        flipped(value_b), key_b * decay_out
    )
    carry_keep = 1.0 - resets.astype(jnp.float32)
    device_map = jnp.broadcast_to(identity, (attention_lane_count, LANE_FEATURES, LANE_FEATURES))
    device_add = jnp.zeros((attention_lane_count, LANE_FEATURES, LANE_FEATURES), jnp.float32)
    for position in range(block_count):
        masked = step_map[position] * carry_keep[position]
        device_map = product(device_map, masked)
        device_add = product(device_add, masked) + step_add[position]
    seq_count = lax.axis_size("seq")
    longest = seq_count * block_count // 2
    rounds = min(seq_count - 1, (longest + block_count - 2) // block_count)

    def advance(rounds_done, arriving):
        leaving = product(arriving, device_map) + device_add
        return passed_along(leaving, "seq", 1)

    incoming = lax.fori_loop(
        0,
        rounds,
        advance,
        jnp.zeros((attention_lane_count, LANE_FEATURES, LANE_FEATURES), jnp.float32),
    )
    current = incoming
    start_states = []
    for position in range(block_count):
        current = current * carry_keep[position]
        start_states.append(current)
        current = product(current, step_map[position]) + step_add[position]
    stacked = jnp.stack(start_states, axis=0)
    result_lines = output_base + product(queries, flipped(stacked))
    result_lines = jnp.swapaxes(result_lines, 1, 2).reshape(
        row_count, attention_lane_count, LANE_FEATURES
    )
    return ending_result(
        result_lines,
        acceptor_lines,
        adjusted_address,
        payload_entries,
        extra_reward_coefs,
        cluster_normalize_multiplier,
    )


def solution(mesh):
    placed = (
        P(("seq", "head"), None),
        P(),
        P("seq", "head"),
        P("seq", "head"),
        P("seq", "head"),
        P("head"),
        P(),
        P(None, "head"),
        P("head"),
        P(),
        P(None, "head"),
        P("head"),
        P("head"),
        P("head"),
        P("head"),
        P(),
    )
    return jax.shard_map(
        per_device, mesh=mesh, in_specs=placed, out_specs=P("seq", "head"), check_vma=False
    )
```

profile of v0, /device:TPU:16, one launch (start us, length us, event | category | flops | bytes accessed | tf_op | source)
XLA Modules:
  0.0 833.2 jit_solution(749002571886270227)
XLA Ops:
  10.1 21.2 %all-gather.5.cloned.1.call-done = bf16[128,4096]{1,0:T(8,128)(2,1)} async-done(((bf16[64,4096]{1,0:T(8,128)(2,1)}), bf16[128,4096]{1,0:T(8,128)(2,1)}) %all-gather.5.cloned.1.call-update) | async-done | bytes 1048592 | tf_op jit(solution)/shard_map/all_gather | solution.py:169
  52.2 106.9 %all-gather.9.cloned.1.call-done = bf16[4096,2048]{1,0:T(8,128)(2,1)} async-done(((bf16[256,2048]{1,0:T(8,128)(2,1)}), bf16[4096,2048]{1,0:T(8,128)(2,1)}) %all-gather.9.cloned.1.call-update) | async-done | bytes 16777232 | tf_op jit(solution)/shard_map/all_gather | solution.py:181
  159.0 10.5 %fusion.85 = (f32[128,2048]{1,0:T(8,128)}, f32[128,2048]{1,0:T(8,128)}, f32[128,2048]{1,0:T(8,128)S(1)}) fusion(f32[2048]{0:T(1024)S(1)} %copy-done.40, bf16[4096,2048]{1,0:T(8,128)(2,1)} %all-gather.9.cloned.1.call-done, bf16[128,4096]{1,0:T(8,128)(2,1)} %all-gather.5.cloned.1.call-done, f32[4096]{0:T(1024)S(1)} %bitcast.131, ...), kind=kOutput, calls=%fused_computation.135 | convolution fusion | flops 2153775104 | bytes 22044800 | tf_op jit(solution)/shard_map/dot_general | solution.py:184
  173.0 112.8 %all-gather.7.cloned.1.call-done = bf16[4096,2048]{1,0:T(8,128)(2,1)} async-done(((bf16[256,2048]{1,0:T(8,128)(2,1)}), bf16[4096,2048]{1,0:T(8,128)(2,1)}) %all-gather.7.cloned.1.call-update) | async-done | bytes 16777232 | tf_op jit(solution)/shard_map/all_gather | solution.py:180
  285.8 9.1 %fusion.59 = f32[128,2048]{1,0:T(8,128)S(1)} fusion(bf16[4096,2048]{1,0:T(8,128)(2,1)} %all-gather.7.cloned.1.call-done, bf16[128,4096]{1,0:T(8,128)(2,1)} %all-gather.5.cloned.1.call-done, f32[4096]{0:T(1024)S(1)} %bitcast.130, bf16[127,4096]{1,0:T(8,128)(2,1)} %bitcast.137, bf16[1,4096]{1,0:T(2,128)(2,1)S(1)} %collective-permute-done.1, ...), kind=kOutput, calls=%fused_computation.85 | convolution fusion | flops 2153250816 | bytes 19939456 | tf_op jit(solution)/shard_map/dot_general | solution.py:183
  303.4 5.0 copy_multiply_fusion
  308.4 6.3 bitcast_multiply_fusion.3
  316.0 6.0 fusion.72
  322.1 4.2 copy.220
  326.3 11.7 %fusion.84 = f32[2,32,64,64]{3,2,1,0:T(8,128)} fusion(f32[2,32,64,64]{3,2,1,0:T(8,128)} %copy-done.16, f32[2,32,64,64]{3,1,2,0:T(8,128)S(1)} %fusion.30, f32[2,64,32,64]{3,2,1,0:T(8,128)} %reshape.155, f32[2,64,32]{1,2,0:T(8,128)S(1)} %copy.211, f32[2,64,32,64]{3,2,1,0:T(8,128)} %reshape.154), kind=kOutput, calls=%fused_computation.134 | convolution fusion | flops 202375168 | bytes 5259264 | tf_op jit(solution)/shard_map/dot_general | solution.py:22
  338.0 4.2 copy.217
  342.3 9.9 %broadcast_select_fusion = (f32[2,32,64,64]{1,3,2,0:T(8,128)}, f32[2,32,1,64,64]{1,4,3,2,0:T(8,128)}) fusion(f32[2,32,64,64]{1,3,2,0:T(8,128)} %copy.220, pred[64,64]{1,0:T(8,128)(4,1)S(1)} %get-tuple-element.75, f32[64,64]{1,0:T(8,128)S(1)} %get-tuple-element.78, f32[2,32,64,64]{1,3,2,0:T(8,128)} %copy.217, f32[64,64]{1,0:T(8,128)S(1)} %get-tuple-element.77, ...), kind=kLoop, calls=%fused_computation.59 | loop fusion | flops 1310720 | bytes 4235264 | tf_op jit(solution)/shard_map/jit(_where)/select_n | solution.py:136
  352.2 134.2 %custom-call.4 = f32[2,32,1,64,64]{1,3,4,2,0:T(8,128)} custom-call(f32[2,32,1,64,64]{1,4,3,2,0:T(8,128)} %get-tuple-element.67), custom_call_target="InvertDiagBlocksLowerTriangular" | custom-call | tf_op jit(solution)/shard_map/jit(_solve_triangular)/vmap(vmap())/triangular_solve | solution.py:216
  486.3 5.2 copy.224
  491.6 4.3 copy.222
  495.8 10.9 %fusion.71 = f32[2,32,64,64]{3,2,1,0:T(8,128)} fusion(f32[2,64,32,64]{3,1,2,0:T(8,128)} %copy-done.5, f32[2,32,64,64]{3,1,2,0:T(8,128)S(1)} %fusion.30, f32[2,64,32,64]{3,2,1,0:T(8,128)} %reshape_reshape.9), kind=kOutput, calls=%fused_computation.103 | convolution fusion | flops 202113024 | bytes 4194304 | tf_op jit(solution)/shard_map/dot_general | solution.py:22
  506.8 10.5 %fusion.83 = f32[2,32,64,64]{3,2,1,0:T(8,128)} fusion(f32[2,64,32,64]{3,2,1,0:T(8,128)S(1)} %copy-done.9, f32[2,32,64,64]{3,1,2,0:T(8,128)S(1)} %fusion.30, f32[2,64,32,64]{3,2,1,0:T(8,128)S(1)} %copy-done.12, f32[2,64,32]{1,2,0:T(8,128)S(1)} %copy.211, f32[2,64,32,64]{3,2,1,0:T(8,128)S(1)} %copy-done.23), kind=kOutput, calls=%fused_computation.133 | convolution fusion | flops 202637312 | bytes 5259264 | tf_op jit(solution)/shard_map/dot_general | solution.py:22
  517.4 9.1 %fusion.51 = f32[128,2048]{1,0:T(8,128)S(1)} fusion(bf16[4096,2048]{1,0:T(8,128)(2,1)} %all-gather.11.cloned.1.call-done, bf16[128,4096]{1,0:T(8,128)(2,1)} %all-gather.5.cloned.1.call-done, f32[4096]{0:T(1024)S(1)} %bitcast.129, bf16[127,4096]{1,0:T(8,128)(2,1)} %bitcast.138, bf16[1,4096]{1,0:T(2,128)(2,1)S(1)} %collective-permute-done.1, ...), kind=kOutput, calls=%fused_computation.83 | convolution fusion | flops 2153250816 | bytes 19939456 | tf_op jit(solution)/shard_map/dot_general | solution.py:185
  532.1 5.7 fusion.26
  541.6 5.0 fusion.34
  546.6 3.9 copy.233
  561.1 5.9 fusion.24
  567.0 5.7 fusion.44
  590.1 167.1 %while.10 = (s32[]{:T(128)}, f32[32,64,64]{2,1,0:T(8,128)S(1)}, f32[32,64,64]{2,1,0:T(8,128)}, f32[32,64,64]{2,1,0:T(8,128)}, s32[]{:T(128)}) while((s32[]{:T(128)}, f32[32,64,64]{2,1,0:T(8,128)S(1)}, f32[32,64,64]{2,1,0:T(8,128)}, f32[32,64,64]{2,1,0:T(8,128)}, s32[]{:T(128)}) %tuple.38), condition=%wide.region_5.6_spmd, body=%wide.region_4.5_spmd.sunk | while | flops 100794368 | bytes 4194405 | solution.py:244
  590.1 3.7 convolution_add_fusion.7
  595.8 15.2 %collective-permute-done = f32[32,64,64]{2,1,0:T(8,128)S(1)} collective-permute-done((f32[32,64,64]{2,1,0:T(8,128)}, f32[32,64,64]{2,1,0:T(8,128)S(1)}, u32[]{:S(2)}, u32[]{:S(2)}) %collective-permute-start) | collective-permute-done | bytes 524320 | tf_op jit(solution)/shard_map/while/body/eval_jaxpr/ppermute | solution.py:18
  611.0 3.7 convolution_add_fusion.7
  616.6 15.3 %collective-permute-done = f32[32,64,64]{2,1,0:T(8,128)S(1)} collective-permute-done((f32[32,64,64]{2,1,0:T(8,128)}, f32[32,64,64]{2,1,0:T(8,128)S(1)}, u32[]{:S(2)}, u32[]{:S(2)}) %collective-permute-start) | collective-permute-done | bytes 524320 | tf_op jit(solution)/shard_map/while/body/eval_jaxpr/ppermute | solution.py:18
  637.4 15.3 %collective-permute-done = f32[32,64,64]{2,1,0:T(8,128)S(1)} collective-permute-done((f32[32,64,64]{2,1,0:T(8,128)}, f32[32,64,64]{2,1,0:T(8,128)S(1)}, u32[]{:S(2)}, u32[]{:S(2)}) %collective-permute-start) | collective-permute-done | bytes 524320 | tf_op jit(solution)/shard_map/while/body/eval_jaxpr/ppermute | solution.py:18
  652.7 3.7 convolution_add_fusion.7
  658.3 15.3 %collective-permute-done = f32[32,64,64]{2,1,0:T(8,128)S(1)} collective-permute-done((f32[32,64,64]{2,1,0:T(8,128)}, f32[32,64,64]{2,1,0:T(8,128)S(1)}, u32[]{:S(2)}, u32[]{:S(2)}) %collective-permute-start) | collective-permute-done | bytes 524320 | tf_op jit(solution)/shard_map/while/body/eval_jaxpr/ppermute | solution.py:18
  673.6 3.7 convolution_add_fusion.7
  679.2 15.3 %collective-permute-done = f32[32,64,64]{2,1,0:T(8,128)S(1)} collective-permute-done((f32[32,64,64]{2,1,0:T(8,128)}, f32[32,64,64]{2,1,0:T(8,128)S(1)}, u32[]{:S(2)}, u32[]{:S(2)}) %collective-permute-start) | collective-permute-done | bytes 524320 | tf_op jit(solution)/shard_map/while/body/eval_jaxpr/ppermute | solution.py:18
  694.5 3.7 convolution_add_fusion.7
  700.1 15.3 %collective-permute-done = f32[32,64,64]{2,1,0:T(8,128)S(1)} collective-permute-done((f32[32,64,64]{2,1,0:T(8,128)}, f32[32,64,64]{2,1,0:T(8,128)S(1)}, u32[]{:S(2)}, u32[]{:S(2)}) %collective-permute-start) | collective-permute-done | bytes 524320 | tf_op jit(solution)/shard_map/while/body/eval_jaxpr/ppermute | solution.py:18
  721.0 15.3 %collective-permute-done = f32[32,64,64]{2,1,0:T(8,128)S(1)} collective-permute-done((f32[32,64,64]{2,1,0:T(8,128)}, f32[32,64,64]{2,1,0:T(8,128)S(1)}, u32[]{:S(2)}, u32[]{:S(2)}) %collective-permute-start) | collective-permute-done | bytes 524320 | tf_op jit(solution)/shard_map/while/body/eval_jaxpr/ppermute | solution.py:18
  736.3 3.7 convolution_add_fusion.7
  741.8 15.3 %collective-permute-done = f32[32,64,64]{2,1,0:T(8,128)S(1)} collective-permute-done((f32[32,64,64]{2,1,0:T(8,128)}, f32[32,64,64]{2,1,0:T(8,128)S(1)}, u32[]{:S(2)}, u32[]{:S(2)}) %collective-permute-start) | collective-permute-done | bytes 524320 | tf_op jit(solution)/shard_map/while/body/eval_jaxpr/ppermute | solution.py:18
  759.0 4.6 fusion.49
  763.6 3.9 copy.227
  767.5 3.9 copy.215
  771.4 6.5 broadcast_select_fusion.1
  777.9 4.1 copy.225
  782.0 5.7 fusion.36
  787.7 4.5 copy.228
  792.3 5.8 fusion.28
  798.2 6.2 fusion.20
  804.4 4.4 fusion.90
  (172 shorter events, 117.1 us)
Async XLA Ops:
  6.5 31.6 %copy-start = (bf16[4096,128]{1,0:T(8,128)(2,1)S(1)}, bf16[4096,128]{1,0:T(8,128)(2,1)}, u32[]{:S(2)}) copy-start(bf16[4096,128]{1,0:T(8,128)(2,1)} %param.27) | copy-start | bytes 3145732
  6.5 2.8 copy-start.41
  6.5 3.5 copy-start.34
  6.5 28.1 %copy-start.36 = (f32[2048]{0:T(1024)S(1)}, f32[2048]{0:T(1024)}, u32[]{:S(2)}) copy-start(f32[2048]{0:T(1024)} %param.31) | copy-start | bytes 24580
  6.5 28.2 %copy-start.37 = (f32[2048]{0:T(1024)S(1)}, f32[2048]{0:T(1024)}, u32[]{:S(2)}) copy-start(f32[2048]{0:T(1024)} %param.30) | copy-start | bytes 24580
  6.5 31.6 %copy-start.38 = (f32[2048]{0:T(1024)S(1)}, f32[2048]{0:T(1024)}, u32[]{:S(2)}) copy-start(f32[2048]{0:T(1024)} %param.26) | copy-start | bytes 24580
  6.6 24.7 %all-gather.5.cloned.1.call-start = ((), (), s32[]{:S(2)}) async-start(), calls=%async_computation | async-start | bytes 1572864 | tf_op jit(solution)/shard_map/all_gather | solution.py:169
  7.3 151.7 %all-gather.9.cloned.1.call-start = ((), (), s32[]{:S(2)}) async-start(), calls=%async_computation.2 | async-start | bytes 17825792 | tf_op jit(solution)/shard_map/all_gather | solution.py:181
  8.0 277.8 %all-gather.7.cloned.1.call-start = ((), (), s32[]{:S(2)}) async-start(), calls=%async_computation.1 | async-start | bytes 17825792 | tf_op jit(solution)/shard_map/all_gather | solution.py:180
  8.8 508.6 %all-gather.11.cloned.1.call-start = ((), (), s32[]{:S(2)}) async-start(), calls=%async_computation.3 | async-start | bytes 17825792 | tf_op jit(solution)/shard_map/all_gather | solution.py:182
  32.2 6.0 collective-permute-start.1
  50.4 108.6 %copy-start.40 = (f32[2048]{0:T(1024)S(1)}, f32[2048]{0:T(1024)}, u32[]{:S(2)}) copy-start(f32[2048]{0:T(1024)} %param.29) | copy-start | bytes 24580
  303.4 5.0 copy-start.11
  303.4 5.0 copy-start.15
  303.4 5.0 copy-start.22
  308.4 6.3 copy-start.5
  495.8 11.0 %copy-start.9 = (f32[2,64,32,64]{3,2,1,0:T(8,128)S(1)}, f32[2,64,32,64]{3,2,1,0:T(8,128)}, u32[]{:S(2)}) copy-start(f32[2,64,32,64]{3,2,1,0:T(8,128)} %reshape_reshape.9) | copy-start | bytes 3145732
  495.8 11.0 %copy-start.12 = (f32[2,64,32,64]{3,2,1,0:T(8,128)S(1)}, f32[2,64,32,64]{3,2,1,0:T(8,128)}, u32[]{:S(2)}) copy-start(f32[2,64,32,64]{3,2,1,0:T(8,128)} %reshape.155) | copy-start | bytes 3145732
  495.8 11.0 %copy-start.23 = (f32[2,64,32,64]{3,2,1,0:T(8,128)S(1)}, f32[2,64,32,64]{3,2,1,0:T(8,128)}, u32[]{:S(2)}) copy-start(f32[2,64,32,64]{3,2,1,0:T(8,128)} %reshape.154) | copy-start | bytes 3145732
  526.5 5.6 copy-start.29
  532.1 5.8 copy-start.17
  532.1 5.8 copy-start.24
  537.8 3.8 copy-start.13
  554.5 3.3 copy-start.6
  561.1 5.9 copy-start.3
  561.1 5.9 copy-start.14
  567.0 5.7 copy-start.7
  582.8 2.7 copy-start.20
  582.8 2.7 copy-start.28
  585.5 2.2 copy-start.18
  593.8 17.2 %collective-permute-start = (f32[32,64,64]{2,1,0:T(8,128)}, f32[32,64,64]{2,1,0:T(8,128)S(1)}, u32[]{:S(2)}, u32[]{:S(2)}) collective-permute-start(f32[32,64,64]{2,1,0:T(8,128)} %convolution_add_fusion.7), channel_id=1, source_target_pairs={{0,2},{2,4},{4,6},{6,8},{8,10},{10,12},{12,14},{14,16},{16,18},{18... | collective-permute-start | bytes 1572872 | tf_op jit(solution)/shard_map/while/body/eval_jaxpr/ppermute | solution.py:18
  614.6 17.2 %collective-permute-start = (f32[32,64,64]{2,1,0:T(8,128)}, f32[32,64,64]{2,1,0:T(8,128)S(1)}, u32[]{:S(2)}, u32[]{:S(2)}) collective-permute-start(f32[32,64,64]{2,1,0:T(8,128)} %convolution_add_fusion.7), channel_id=1, source_target_pairs={{0,2},{2,4},{4,6},{6,8},{8,10},{10,12},{12,14},{14,16},{16,18},{18... | collective-permute-start | bytes 1572872 | tf_op jit(solution)/shard_map/while/body/eval_jaxpr/ppermute | solution.py:18
  635.5 17.2 %collective-permute-start = (f32[32,64,64]{2,1,0:T(8,128)}, f32[32,64,64]{2,1,0:T(8,128)S(1)}, u32[]{:S(2)}, u32[]{:S(2)}) collective-permute-start(f32[32,64,64]{2,1,0:T(8,128)} %convolution_add_fusion.7), channel_id=1, source_target_pairs={{0,2},{2,4},{4,6},{6,8},{8,10},{10,12},{12,14},{14,16},{16,18},{18... | collective-permute-start | bytes 1572872 | tf_op jit(solution)/shard_map/while/body/eval_jaxpr/ppermute | solution.py:18
  656.4 17.2 %collective-permute-start = (f32[32,64,64]{2,1,0:T(8,128)}, f32[32,64,64]{2,1,0:T(8,128)S(1)}, u32[]{:S(2)}, u32[]{:S(2)}) collective-permute-start(f32[32,64,64]{2,1,0:T(8,128)} %convolution_add_fusion.7), channel_id=1, source_target_pairs={{0,2},{2,4},{4,6},{6,8},{8,10},{10,12},{12,14},{14,16},{16,18},{18... | collective-permute-start | bytes 1572872 | tf_op jit(solution)/shard_map/while/body/eval_jaxpr/ppermute | solution.py:18
  677.3 17.2 %collective-permute-start = (f32[32,64,64]{2,1,0:T(8,128)}, f32[32,64,64]{2,1,0:T(8,128)S(1)}, u32[]{:S(2)}, u32[]{:S(2)}) collective-permute-start(f32[32,64,64]{2,1,0:T(8,128)} %convolution_add_fusion.7), channel_id=1, source_target_pairs={{0,2},{2,4},{4,6},{6,8},{8,10},{10,12},{12,14},{14,16},{16,18},{18... | collective-permute-start | bytes 1572872 | tf_op jit(solution)/shard_map/while/body/eval_jaxpr/ppermute | solution.py:18
  698.2 17.2 %collective-permute-start = (f32[32,64,64]{2,1,0:T(8,128)}, f32[32,64,64]{2,1,0:T(8,128)S(1)}, u32[]{:S(2)}, u32[]{:S(2)}) collective-permute-start(f32[32,64,64]{2,1,0:T(8,128)} %convolution_add_fusion.7), channel_id=1, source_target_pairs={{0,2},{2,4},{4,6},{6,8},{8,10},{10,12},{12,14},{14,16},{16,18},{18... | collective-permute-start | bytes 1572872 | tf_op jit(solution)/shard_map/while/body/eval_jaxpr/ppermute | solution.py:18
  719.0 17.2 %collective-permute-start = (f32[32,64,64]{2,1,0:T(8,128)}, f32[32,64,64]{2,1,0:T(8,128)S(1)}, u32[]{:S(2)}, u32[]{:S(2)}) collective-permute-start(f32[32,64,64]{2,1,0:T(8,128)} %convolution_add_fusion.7), channel_id=1, source_target_pairs={{0,2},{2,4},{4,6},{6,8},{8,10},{10,12},{12,14},{14,16},{16,18},{18... | collective-permute-start | bytes 1572872 | tf_op jit(solution)/shard_map/while/body/eval_jaxpr/ppermute | solution.py:18
  739.9 17.2 %collective-permute-start = (f32[32,64,64]{2,1,0:T(8,128)}, f32[32,64,64]{2,1,0:T(8,128)S(1)}, u32[]{:S(2)}, u32[]{:S(2)}) collective-permute-start(f32[32,64,64]{2,1,0:T(8,128)} %convolution_add_fusion.7), channel_id=1, source_target_pairs={{0,2},{2,4},{4,6},{6,8},{8,10},{10,12},{12,14},{14,16},{16,18},{18... | collective-permute-start | bytes 1572872 | tf_op jit(solution)/shard_map/while/body/eval_jaxpr/ppermute | solution.py:18
  792.2 5.9 copy-start.10
  792.2 5.9 copy-start.21
  792.2 5.9 copy-start.26
  792.3 5.9 copy-start.27
  798.2 6.2 copy-start.4
  798.2 6.2 copy-start.8
  819.6 3.8 copy-start.30
  819.6 3.8 copy-start.31
  819.6 3.8 copy-start.35
  820.7 5.8 copy-start.1
  (7 other events, 10.4 us)
Sparse Core Ops, SparseCore 0:
  8.9 22.3 all-gather.4
  33.5 125.5 all-gather.8
  161.2 124.5 all-gather.6
  287.8 124.5 all-gather.10
where the time goes:
time: 844 us; the launch traced here: 833 us
  waiting for transfers between devices  369 us (44%)
  other arithmetic  180 us (21%)
  matrix products  164 us (19%)
  local copies, waits for them, and re-layouts  88.6 us (10%)
  starting transfers between devices  17.5 us (2%)
  between operations  13.9 us (2%)
    another operation x2, other arithmetic, per_device(): jax.scipy.linalg.solve_triangular(solve_matrix, right_side, lower=True, u...  134 us
    dot_general x25, matrix products, product(): return jnp.matmul(left, right, precision=exact_precision)  127 us
    ppermute x9, waiting for transfers between devices, passed_along(): return lax.ppermute(block, axis, route)  126 us
    all_gather x1, waiting for transfers between devices, per_device(): whole_recept = lax.all_gather(acceptor_projector, 'seq', axis=0, tiled=True)  113 us
    all_gather x1, waiting for transfers between devices, per_device(): whole_key = lax.all_gather(address_projector, 'seq', axis=0, tiled=True)  107 us
    all_gather x1, waiting for transfers between devices, per_device(): gathered = lax.all_gather(packed_inputs_slab, 'head', axis=0, tiled=True)  21.2 us
    dot_general x5, local copies, waits for them, and re-layouts, product(): return jnp.matmul(left, right, precision=exact_precision)  20.1 us
    ppermute x9, starting transfers between devices, passed_along(): return lax.ppermute(block, axis, route)  17.3 us
  transfers between devices with their start and end apart: 13, of which 12 were waited for; matrix products, arithmetic and copies ran while one was open for 31% of the time, Pallas kernels for 0%

commit v1 on v0

--- a/solution.py
+++ b/solution.py
@@ -1,6 +1,10 @@
+import functools
+
 import jax
 import jax.numpy as jnp
 from jax import lax
+from jax.experimental import pallas as pl
+from jax.experimental.pallas import tpu as pltpu
 from jax.sharding import PartitionSpec as P
 
 LANE_FEATURES = 64
@@ -268,6 +272,248 @@
     )
 
 
+PAIR = 2 * LANE_FEATURES
+UNROLL = 4
+
+
+def split(array):
+    high = array.astype(jnp.bfloat16)
+    low = (array - high.astype(jnp.float32)).astype(jnp.bfloat16)
+    return high, low
+
+
+def contract(left, right, left_dim, right_dim):
+    dims = (((left_dim,), (right_dim,)), ((), ()))
+    dot = functools.partial(
+        lax.dot_general, dimension_numbers=dims, preferred_element_type=jnp.float32
+    )
+    wide_left = jnp.concatenate(left, axis=left_dim)
+    wide_right = jnp.concatenate([right[0], right[0]], axis=right_dim)
+    return dot(wide_left, wide_right) + dot(left[0], right[1])
+
+
+def mm(left, right):
+    return contract(left, right, 1, 0)
+
+
+def mm_nt(left, right):
+    return contract(left, right, 1, 1)
+
+
+def mm_tn(left, right):
+    return contract(left, right, 0, 0)
+
+
+def mixing_kernel(
+    keep_ref,
+    recept_ref,
+    keyed_ref,
+    value_ref,
+    decay_ref,
+    icl_ref,
+    params_ref,
+    out_ref,
+    state_ref,
+):
+    step = pl.program_id(1)
+
+    @pl.when(step == 0)
+    def _():
+        state_ref[...] = jnp.zeros_like(state_ref)
+
+    def iota(shape, dim):
+        return lax.broadcasted_iota(jnp.int32, shape, dim)
+
+    square = (PAIR, PAIR)
+    row, col = iota(square, 0), iota(square, 1)
+    same_head = row // LANE_FEATURES == col // LANE_FEATURES
+    ones_head = jnp.where(same_head, 1.0, 0.0).astype(jnp.bfloat16)
+    first_head = iota((SPAN, PAIR), 1) < LANE_FEATURES
+    strict = row > col
+    on_or_below = row >= col
+    eye = jnp.where(row == col, 1.0, 0.0)
+    triangle = jnp.where(iota((SPAN, SPAN), 0) >= iota((SPAN, SPAN), 1), 1.0, 0.0).astype(
+        jnp.bfloat16
+    )
+
+    def head_sum(array):
+        high, low = split(array)
+        return jnp.dot(high, ones_head, preferred_element_type=jnp.float32) + jnp.dot(
+            low, ones_head, preferred_element_type=jnp.float32
+        )
+
+    def running_sum(array):
+        high, low = split(array)
+        rest = (array - high.astype(jnp.float32) - low.astype(jnp.float32)).astype(jnp.bfloat16)
+        dot = functools.partial(jnp.dot, preferred_element_type=jnp.float32)
+        return dot(triangle, high) + (dot(triangle, low) + dot(triangle, rest))
+
+    def stack(array):
+        zero = jnp.zeros_like(array)
+        return jnp.concatenate(
+            [jnp.where(first_head, array, zero), jnp.where(first_head, zero, array)], axis=0
+        )
+
+    def param(index):
+        return params_ref[index : index + 1, :]
+
+    before_unit, strength, reward, gain = param(0), param(1), param(2), param(3)
+    recept, keyed, value = recept_ref[...], keyed_ref[...], value_ref[...]
+    log_decay = -decay_limit * jax.nn.sigmoid(decay_ref[...])
+    icl = jax.nn.sigmoid(icl_ref[...])
+    scaled = keyed * before_unit
+    unit_key = scaled / jnp.sqrt(head_sum(scaled * scaled) + norm_eps)
+    key_mod = keyed * (1.0 + (icl - 1.0) * strength)
+    beta = unit_key * icl
+    alpha = -unit_key
+    bonus = head_sum(recept * key_mod * reward) * value
+
+    terms = []
+    for index in range(recept.shape[0] // SPAN):
+        rows = slice(index * SPAN, (index + 1) * SPAN)
+        decay_b = log_decay[rows]
+        log_sums = running_sum(decay_b)
+        decay_in = jnp.exp(log_sums)
+        inverse = jnp.exp(-log_sums)
+        decay_out = jnp.exp(log_sums[SPAN - 1 :] - log_sums)
+        alpha_s = stack(alpha[rows] * jnp.exp(log_sums - decay_b))
+        recept_s = stack(recept[rows] * decay_in)
+        left = jnp.concatenate([alpha_s, recept_s], axis=0)
+        right = jnp.concatenate(
+            [stack(beta[rows] * inverse), stack(key_mod[rows] * inverse)], axis=0
+        )
+        scores = mm_nt(split(left), split(right))
+        within = jnp.where(strict, scores[:PAIR, :PAIR], 0.0)
+        key_read = jnp.where(strict, scores[:PAIR, PAIR:], 0.0)
+        out_beta = jnp.where(on_or_below, scores[PAIR:, :PAIR], 0.0)
+        out_key = jnp.where(on_or_below, scores[PAIR:, PAIR:], 0.0)
+        value_s = split(stack(value[rows]))
+        from_value = mm(split(jnp.concatenate([key_read, out_key], axis=0)), value_s)
+        solver = eye
+        size = 1
+        while size < SPAN:
+            pair_mask = jnp.logical_and(
+                row // (2 * size) == col // (2 * size), row // size != col // size
+            )
+            corner = jnp.where(pair_mask, within, 0.0)
+            if size == 1:
+                solver = solver + corner
+            else:
+                halves = split(solver)
+                solver = solver + mm(halves, split(mm(split(corner), halves)))
+            size *= 2
+        right_side = jnp.concatenate([alpha_s, from_value[:PAIR]], axis=1)
+        reads = mm(split(solver), split(right_side))
+        reads_split = split(reads)
+        seen = mm(split(out_beta), reads_split)
+        queries = recept_s + seen[:, :PAIR]
+        base = seen[:, PAIR:] + from_value[PAIR:]
+        beta_out = split(stack(beta[rows] * decay_out))
+        key_out = split(stack(key_mod[rows] * decay_out))
+        moved = mm_tn(reads_split, beta_out)
+        step_map = jnp.where(row == col, decay_in[SPAN - 1 :], 0.0) + moved[:PAIR]
+        step_add = moved[PAIR:] + mm_tn(value_s, key_out)
+        terms.append((split(queries), base, split(step_map), step_add))
+
+    state = state_ref[...]
+    results = []
+    for index, (queries, base, step_map, step_add) in enumerate(terms):
+        state = split(state * keep_ref[step * len(terms) + index])
+        result = base + mm_nt(queries, state)
+        results.append(result[:SPAN] + result[SPAN:])
+        state = mm(state, step_map) + step_add
+    state_ref[...] = state
+
+    lines = jnp.concatenate(results, axis=0)
+    centered = lines - head_sum(lines) * (1.0 / LANE_FEATURES)
+    spread = head_sum(centered * centered) * (1.0 / LANE_FEATURES)
+    out_ref[...] = (centered / jnp.sqrt(spread + norm_eps) * gain + bonus).astype(jnp.bfloat16)
+
+
+def mixed_heads(keep, recept, keyed, value, decay_in, icl_in, params):
+    row_count, columns = recept.shape
+    block_count = row_count // SPAN
+    unroll = UNROLL if block_count % UNROLL == 0 else 1
+    rows = unroll * SPAN
+    line = pl.BlockSpec((rows, PAIR), lambda pair, step: (step, pair))
+    return pl.pallas_call(
+        mixing_kernel,
+        grid=(columns // PAIR, block_count // unroll),
+        in_specs=[pl.BlockSpec(memory_space=pltpu.SMEM)]
+        + [line] * 5
+        + [pl.BlockSpec((params.shape[0], PAIR), lambda pair, step: (0, pair))],
+        out_specs=line,
+        out_shape=jax.ShapeDtypeStruct((row_count, columns), jnp.bfloat16),
+        scratch_shapes=[pltpu.VMEM((PAIR, PAIR), jnp.float32)],
+    )(keep, recept, keyed, value, decay_in, icl_in, params)
+
+
+def by_heads(
+    packed_inputs_slab,
+    lagged_blend_coefs,
+    acceptor_projector,
+    address_projector,
+    payload_projector,
+    fading_offset_entry,
+    fading_left_matrix,
+    fading_right_matrix,
+    learning_rate_offset,
+    learning_left_matrix,
+    learning_right_matrix,
+    address_before_unitize,
+    address_learning_strength,
+    extra_reward_coefs,
+    cluster_normalize_multiplier,
+    paper_spans_sizes,
+):
+    seq_count = lax.axis_size("seq")
+    columns = acceptor_projector.shape[1] // seq_count
+    start = lax.axis_index("seq") * columns
+
+    def mine(array):
+        return lax.dynamic_slice_in_dim(array, start, columns, axis=array.ndim - 1)
+
+    gathered = lax.all_gather(packed_inputs_slab, ("seq", "head"), axis=0, tiled=True)
+    own_recept, own_key, own_value = [
+        lax.all_to_all(array, "seq", 1, 0, tiled=True)
+        for array in (acceptor_projector, address_projector, payload_projector)
+    ]
+    row_count = gathered.shape[0]
+    block_count = row_count // SPAN
+    doc_starts = jnp.cumsum(paper_spans_sizes) - paper_spans_sizes
+    span_ids = jnp.arange(block_count, dtype=jnp.int32)
+    resets = jnp.any(doc_starts[None, :] == span_ids[:, None], axis=1)
+    row_start = jnp.logical_and(jnp.arange(row_count) % SPAN == 0, jnp.repeat(resets, SPAN))
+    earlier = jnp.concatenate([jnp.zeros_like(gathered[:1]), gathered[:-1]], axis=0)
+    earlier = jnp.where(row_start[:, None], jnp.zeros_like(earlier), earlier)
+    x_recept, x_decay, x_key, x_value, x_icl = mixed_inputs(gathered, earlier, lagged_blend_coefs)
+
+    def dot(left, right):
+        return jnp.dot(left, right, preferred_element_type=jnp.float32)
+
+    recept = dot(x_recept, own_recept)
+    keyed = dot(x_key, own_key)
+    value = dot(x_value, own_value)
+    decay_low = jnp.tanh(dot(x_decay, fading_left_matrix)).astype(jnp.bfloat16)
+    icl_low = dot(x_icl, learning_left_matrix).astype(jnp.bfloat16)
+    decay_in = mine(fading_offset_entry) + dot(decay_low, mine(fading_right_matrix))
+    icl_in = mine(learning_rate_offset) + dot(icl_low, mine(learning_right_matrix))
+    params = jnp.stack(
+        [
+            mine(array)
+            for array in (
+                address_before_unitize,
+                address_learning_strength,
+                extra_reward_coefs,
+                cluster_normalize_multiplier,
+            )
+        ]
+    )
+    keep = 1.0 - resets.astype(jnp.float32)
+    lines = mixed_heads(keep, recept, keyed, value, decay_in, icl_in, params)
+    return lax.all_to_all(lines, "seq", 0, 1, tiled=True)
+
+
 def solution(mesh):
     placed = (
         P(("seq", "head"), None),
@@ -287,6 +533,16 @@
         P("head"),
         P(),
     )
-    return jax.shard_map(
-        per_device, mesh=mesh, in_specs=placed, out_specs=P("seq", "head"), check_vma=False
-    )
+
+    def run(*arrays):
+        width = arrays[2].shape[1] // mesh.shape["head"]
+        whole_pairs = width % (mesh.shape["seq"] * PAIR) == 0
+        return jax.shard_map(
+            by_heads if whole_pairs else per_device,
+            mesh=mesh,
+            in_specs=placed,
+            out_specs=P("seq", "head"),
+            check_vma=False,
+        )(*arrays)
+
+    return run

time: 844 us -> 423 us (0.50)
  the two profiles are of different devices: /device:TPU:16 before, /device:TPU:0 now
where the time goes in v1:
time: 423 us; the launch traced here: 416 us
  waiting for transfers between devices  132 us (31%)
  matrix products  118 us (28%)
  Pallas kernels  92.1 us (22%)
  starting transfers between devices  23.7 us (6%)
  blocking collectives  18 us (4%)
  local copies, waits for them, and re-layouts  15.8 us (4%)
  between operations  13.7 us (3%)
    dot_general x5, matrix products, dot(): return jnp.dot(left, right, preferred_element_type=jnp.float32)  118 us
    all_to_all x3, waiting for transfers between devices, by_heads(): lax.all_to_all(array, 'seq', 1, 0, tiled=True)  99.9 us
    pallas_call x1, Pallas kernels, mixed_heads(): pl.pallas_call(mixing_kernel, grid=(columns // PAIR, block_count // unrol...  92.1 us
    all_gather x1, waiting for transfers between devices, by_heads(): lax.all_gather(packed_inputs_slab, ('seq', 'head'), axis=0, tiled=True)  31.5 us
    all_to_all x3, starting transfers between devices, by_heads(): lax.all_to_all(array, 'seq', 1, 0, tiled=True)  23.7 us
    all_to_all x1, blocking collectives, by_heads(): return lax.all_to_all(lines, 'seq', 0, 1, tiled=True)  18 us
  transfers between devices with their start and end apart: 4, of which 4 were waited for; matrix products, arithmetic and copies ran while one was open for 4% of the time, Pallas kernels for 0%

profile of v1, /device:TPU:0, one launch (start us, length us, event | category | flops | bytes accessed | tf_op | source)
XLA Modules:
  0.0 416.3 jit_solution(12843155122512979336)
XLA Ops:
  6.5 0.0 copy-start
  6.5 0.0 all-gather.2.cloned.1.call-start
  6.5 0.7 all-gather.2.cloned.1.call-update
  7.3 2.3 copy.26
  9.5 7.4 %all-to-all-start = ((bf16[256,16,128]{0,2,1:T(8,128)(2,1)}), bf16[256,16,128]{0,2,1:T(8,128)(2,1)S(1)}, u32[]{:S(2)}, u32[]{:S(2)}) async-start(bf16[256,16,128]{0,2,1:T(8,128)(2,1)} %bitcast.3), calls=%async_computation | async-start | bytes 2097152 | tf_op jit(solution)/shard_map/all_to_all | solution.py:478
  16.9 2.3 copy.28
  19.2 31.7 %all-to-all-done = bf16[256,16,128]{0,2,1:T(8,128)(2,1)S(1)} async-done(((bf16[256,16,128]{0,2,1:T(8,128)(2,1)}), bf16[256,16,128]{0,2,1:T(8,128)(2,1)S(1)}, u32[]{:S(2)}, u32[]{:S(2)}) %all-to-all-start) | async-done | bytes 1048608 | tf_op jit(solution)/shard_map/all_to_all | solution.py:478
  50.9 6.9 %all-to-all-start.1 = ((bf16[256,16,128]{0,2,1:T(8,128)(2,1)}), bf16[256,16,128]{0,2,1:T(8,128)(2,1)S(1)}, u32[]{:S(2)}, u32[]{:S(2)}) async-start(bf16[256,16,128]{0,2,1:T(8,128)(2,1)} %bitcast.41), calls=%async_computation.1 | async-start | bytes 2097152 | tf_op jit(solution)/shard_map/all_to_all | solution.py:478
  57.8 2.3 copy.30
  60.0 0.8 reduce-window.9
  60.8 36.8 %all-to-all-done.1 = bf16[256,16,128]{0,2,1:T(8,128)(2,1)S(1)} async-done(((bf16[256,16,128]{0,2,1:T(8,128)(2,1)}), bf16[256,16,128]{0,2,1:T(8,128)(2,1)S(1)}, u32[]{:S(2)}, u32[]{:S(2)}) %all-to-all-start.1) | async-done | bytes 1048608 | tf_op jit(solution)/shard_map/all_to_all | solution.py:478
  97.7 9.4 %all-to-all-start.2 = ((bf16[256,16,128]{0,2,1:T(8,128)(2,1)}), bf16[256,16,128]{0,2,1:T(8,128)(2,1)}, u32[]{:S(2)}, u32[]{:S(2)}) async-start(bf16[256,16,128]{0,2,1:T(8,128)(2,1)} %bitcast.40), calls=%async_computation.2 | async-start | bytes 2097152 | tf_op jit(solution)/shard_map/all_to_all | solution.py:478
  107.1 0.7 bitcast_subtract_fusion
  107.8 0.1 fusion.35
  107.9 0.1 broadcast_in_dim.12
  107.9 0.1 reshape.61
  108.0 0.8 dynamic_slice.24
  108.8 0.8 dynamic_slice.26
  109.6 0.8 dynamic-slice_bitcast_fusion
  110.4 0.8 dynamic-slice_bitcast_fusion.2
  111.1 0.6 pad_maximum_fusion.params_ref
  111.7 0.6 convert_subtract_fusion.1.keep_ref
  112.3 1.3 fusion.38
  113.6 1.3 copy.27
  114.9 0.7 copy.29
  115.6 31.4 %all-to-all-done.2 = bf16[256,16,128]{0,2,1:T(8,128)(2,1)} async-done(((bf16[256,16,128]{0,2,1:T(8,128)(2,1)}), bf16[256,16,128]{0,2,1:T(8,128)(2,1)}, u32[]{:S(2)}, u32[]{:S(2)}) %all-to-all-start.2) | async-done | bytes 1048608 | tf_op jit(solution)/shard_map/all_to_all | solution.py:478
  147.0 1.6 copy.31
  148.6 31.5 %all-gather.2.cloned.1.call-done = bf16[2048,4096]{1,0:T(8,128)(2,1)} async-done(((bf16[64,4096]{1,0:T(8,128)(2,1)}), bf16[2048,4096]{1,0:T(8,128)(2,1)}) %all-gather.2.cloned.1.call-update) | async-done | bytes 16777232 | tf_op jit(solution)/shard_map/all_gather | solution.py:476
  180.2 22.8 %fusion.13.recept_ref = f32[2048,128]{1,0:T(8,128)} fusion(bf16[4096,128]{1,0:T(8,128)(2,1)} %bitcast.44, bf16[2048,4096]{1,0:T(8,128)(2,1)} %all-gather.2.cloned.1.call-done, f32[4096]{0:T(1024)S(1)} %bitcast.50, bf16[2047,4096]{1,0:T(8,128)(2,1)} %bitcast.51, pred[2048]{0:T(1024)(128)(4,1)S(1)} %fusion.34), kind=kOutput, calls=%fused_computation.16 | convolution fusion | flops 2206203904 | bytes 35661824 | tf_op jit(solution)/shard_map/dot_general | solution.py:492
  203.0 23.1 %fusion.11.keyed_ref = f32[2048,128]{1,0:T(8,128)} fusion(bf16[4096,128]{1,0:T(8,128)(2,1)S(1)} %bitcast.43, bf16[2048,4096]{1,0:T(8,128)(2,1)} %all-gather.2.cloned.1.call-done, f32[4096]{0:T(1024)S(1)} %bitcast.49, bf16[2047,4096]{1,0:T(8,128)(2,1)} %bitcast.52, pred[2048]{0:T(1024)(128)(4,1)S(1)} %fusion.34), kind=kOutput, calls=%fused_computation.15 | convolution fusion | flops 2206203904 | bytes 35661824 | tf_op jit(solution)/shard_map/dot_general | solution.py:492
  226.1 23.4 %fusion.9.value_ref = f32[2048,128]{1,0:T(8,128)} fusion(bf16[4096,128]{1,0:T(8,128)(2,1)S(1)} %bitcast.45, bf16[2048,4096]{1,0:T(8,128)(2,1)} %all-gather.2.cloned.1.call-done, f32[4096]{0:T(1024)S(1)} %bitcast.48, bf16[2047,4096]{1,0:T(8,128)(2,1)} %bitcast.53, pred[2048]{0:T(1024)(128)(4,1)S(1)} %fusion.34), kind=kOutput, calls=%fused_computation.14 | convolution fusion | flops 2206203904 | bytes 35661824 | tf_op jit(solution)/shard_map/dot_general | solution.py:492
  249.4 0.0 copy-done
  249.4 0.0 copy-start.1
  249.4 24.4 %convolution_add_fusion.1.decay_ref = f32[2048,128]{1,0:T(8,128)} fusion(bf16[4096,128]{1,0:T(8,128)(2,1)S(1)} %copy-done, bf16[2048,4096]{1,0:T(8,128)(2,1)} %all-gather.2.cloned.1.call-done, f32[4096]{0:T(1024)S(1)} %bitcast.47, f32[128]{0:T(128)S(1)} %dynamic_slice.24, bf16[128,2048]{1,0:T(8,128)(2,1)} %param.23, s32[]{:T(128)S(6)} %select_n.27, ...), kind=kOutput, calls=%fused_computation.18 | convolution fusion | flops 2273837056 | bytes 35703300 | tf_op jit(solution)/shard_map/dot_general | solution.py:492
  273.8 0.0 copy-done.1
  273.9 24.4 %convolution_add_fusion.icl_ref = f32[2048,128]{1,0:T(8,128)} fusion(bf16[4096,128]{1,0:T(8,128)(2,1)S(1)} %copy-done.1, bf16[2048,4096]{1,0:T(8,128)(2,1)} %all-gather.2.cloned.1.call-done, f32[4096]{0:T(1024)S(1)} %bitcast.46, f32[128]{0:T(128)S(1)} %dynamic_slice.26, bf16[128,2048]{1,0:T(8,128)(2,1)} %param.26, s32[]{:T(128)S(6)} %select_n.27, ...), kind=kOutput, calls=%fused_computation.17 | convolution fusion | flops 2273837056 | bytes 35703300 | tf_op jit(solution)/shard_map/dot_general | solution.py:492
  298.3 92.1 %shard_map.154 = bf16[2048,128]{1,0:T(8,128)(2,1)} custom-call(f32[32]{0:T(128)} %convert_subtract_fusion.1.keep_ref, f32[2048,128]{1,0:T(8,128)} %fusion.13.recept_ref, f32[2048,128]{1,0:T(8,128)} %fusion.11.keyed_ref, f32[2048,128]{1,0:T(8,128)} %fusion.9.value_ref, f32[2048,128]{1,0:T(8,128)} %convolution_add_fusion.1.decay_ref, ...), custom_call_target="tpu_custom_call" | custom-call | tf_op jit(solution)/shard_map/pallas_call | solution.py:439
  390.4 18.0 %all_to_all.76 = bf16[16,128,128]{2,1,0:T(8,128)(2,1)S(1)} all-to-all(bf16[16,128,128]{2,1,0:T(8,128)(2,1)} %bitcast.42), channel_id=1, replica_groups=mesh['seq'=16,'head'=2] {'seq'}, dimensions={0} | all-to-all | bytes 1048576 | tf_op jit(solution)/shard_map/all_to_all | solution.py:514
  408.4 0.9 copy_bitcast_fusion
  (1 shorter events, 0.0 us)
Async XLA Ops:
  6.5 242.9 %copy-start = (bf16[4096,128]{1,0:T(8,128)(2,1)S(1)}, bf16[4096,128]{1,0:T(8,128)(2,1)}, u32[]{:S(2)}) copy-start(bf16[4096,128]{1,0:T(8,128)(2,1)} %param.22) | copy-start | bytes 3145732
  6.5 173.6 %all-gather.2.cloned.1.call-start = ((), (), s32[]{:S(2)}) async-start(), calls=%async_computation.4 | async-start | bytes 17301504 | tf_op jit(solution)/shard_map/all_gather | solution.py:476
  9.5 41.3 %all-to-all-start = ((bf16[256,16,128]{0,2,1:T(8,128)(2,1)}), bf16[256,16,128]{0,2,1:T(8,128)(2,1)S(1)}, u32[]{:S(2)}, u32[]{:S(2)}) async-start(bf16[256,16,128]{0,2,1:T(8,128)(2,1)} %bitcast.3), calls=%async_computation | async-start | bytes 2097152 | tf_op jit(solution)/shard_map/all_to_all | solution.py:478
  50.9 46.8 %all-to-all-start.1 = ((bf16[256,16,128]{0,2,1:T(8,128)(2,1)}), bf16[256,16,128]{0,2,1:T(8,128)(2,1)S(1)}, u32[]{:S(2)}, u32[]{:S(2)}) async-start(bf16[256,16,128]{0,2,1:T(8,128)(2,1)} %bitcast.41), calls=%async_computation.1 | async-start | bytes 2097152 | tf_op jit(solution)/shard_map/all_to_all | solution.py:478
  97.7 49.3 %all-to-all-start.2 = ((bf16[256,16,128]{0,2,1:T(8,128)(2,1)}), bf16[256,16,128]{0,2,1:T(8,128)(2,1)}, u32[]{:S(2)}, u32[]{:S(2)}) async-start(bf16[256,16,128]{0,2,1:T(8,128)(2,1)} %bitcast.40), calls=%async_computation.2 | async-start | bytes 2097152 | tf_op jit(solution)/shard_map/all_to_all | solution.py:478
  249.4 24.4 %copy-start.1 = (bf16[4096,128]{1,0:T(8,128)(2,1)S(1)}, bf16[4096,128]{1,0:T(8,128)(2,1)}, u32[]{:S(2)}) copy-start(bf16[4096,128]{1,0:T(8,128)(2,1)} %param.25) | copy-start | bytes 3145732
Sparse Core Ops, SparseCore 0:
  10.2 169.9 all-gather.1

commit v2 on v1

--- a/solution.py
+++ b/solution.py
@@ -296,6 +296,12 @@
     return contract(left, right, 1, 0)
 
 
+def mm_once(left, right):
+    return jnp.dot(
+        left.astype(jnp.bfloat16), right.astype(jnp.bfloat16), preferred_element_type=jnp.float32
+    )
+
+
 def mm_nt(left, right):
     return contract(left, right, 1, 1)
 
@@ -388,7 +394,7 @@
         out_beta = jnp.where(on_or_below, scores[PAIR:, :PAIR], 0.0)
         out_key = jnp.where(on_or_below, scores[PAIR:, PAIR:], 0.0)
         value_s = split(stack(value[rows]))
-        from_value = mm(split(jnp.concatenate([key_read, out_key], axis=0)), value_s)
+        from_value = mm_once(jnp.concatenate([key_read, out_key], axis=0), value_s[0])
         solver = eye
         size = 1
         while size < SPAN:
@@ -399,13 +405,15 @@
             if size == 1:
                 solver = solver + corner
             else:
-                halves = split(solver)
-                solver = solver + mm(halves, split(mm(split(corner), halves)))
+                rounded = solver.astype(jnp.bfloat16)
+                solver = solver + mm_once(rounded, mm_once(corner, rounded))
             size *= 2
+        residual = eye - solver + mm(split(within), split(solver))
+        solver = solver + mm_once(solver, residual)
         right_side = jnp.concatenate([alpha_s, from_value[:PAIR]], axis=1)
         reads = mm(split(solver), split(right_side))
         reads_split = split(reads)
-        seen = mm(split(out_beta), reads_split)
+        seen = mm_once(out_beta, reads_split[0])
         queries = recept_s + seen[:, :PAIR]
         base = seen[:, PAIR:] + from_value[PAIR:]
         beta_out = split(stack(beta[rows] * decay_out))
@@ -413,13 +421,15 @@
         moved = mm_tn(reads_split, beta_out)
         step_map = jnp.where(row == col, decay_in[SPAN - 1 :], 0.0) + moved[:PAIR]
         step_add = moved[PAIR:] + mm_tn(value_s, key_out)
-        terms.append((split(queries), base, split(step_map), step_add))
+        terms.append((queries.astype(jnp.bfloat16), base, split(step_map), step_add))
 
     state = state_ref[...]
     results = []
     for index, (queries, base, step_map, step_add) in enumerate(terms):
         state = split(state * keep_ref[step * len(terms) + index])
-        result = base + mm_nt(queries, state)
+        result = base + lax.dot_general(
+            queries, state[0], (((1,), (1,)), ((), ())), preferred_element_type=jnp.float32
+        )
         results.append(result[:SPAN] + result[SPAN:])
         state = mm(state, step_map) + step_add
     state_ref[...] = state
@@ -484,18 +494,26 @@
     span_ids = jnp.arange(block_count, dtype=jnp.int32)
     resets = jnp.any(doc_starts[None, :] == span_ids[:, None], axis=1)
     row_start = jnp.logical_and(jnp.arange(row_count) % SPAN == 0, jnp.repeat(resets, SPAN))
-    earlier = jnp.concatenate([jnp.zeros_like(gathered[:1]), gathered[:-1]], axis=0)
-    earlier = jnp.where(row_start[:, None], jnp.zeros_like(earlier), earlier)
-    x_recept, x_decay, x_key, x_value, x_icl = mixed_inputs(gathered, earlier, lagged_blend_coefs)
 
     def dot(left, right):
         return jnp.dot(left, right, preferred_element_type=jnp.float32)
 
-    recept = dot(x_recept, own_recept)
-    keyed = dot(x_key, own_key)
-    value = dot(x_value, own_value)
-    decay_low = jnp.tanh(dot(x_decay, fading_left_matrix)).astype(jnp.bfloat16)
-    icl_low = dot(x_icl, learning_left_matrix).astype(jnp.bfloat16)
+    maps = [own_recept, fading_left_matrix, own_key, own_value, learning_left_matrix]
+    current_maps, earlier_maps = [], []
+    for member, matrix in enumerate(maps):
+        coefs = lagged_blend_coefs[member][:, None]
+        wide = matrix.astype(jnp.float32)
+        current_maps.append((wide * (1.0 - coefs)).astype(jnp.bfloat16))
+        earlier_maps.append((wide * coefs).astype(jnp.bfloat16))
+    products = dot(gathered, jnp.concatenate(current_maps + earlier_maps, axis=1))
+    width = products.shape[1] // 2
+    moved = jnp.concatenate([jnp.zeros_like(products[:1, width:]), products[:-1, width:]], axis=0)
+    mixed = products[:, :width] + jnp.where(row_start[:, None], 0.0, moved)
+    ranks = (columns, fading_left_matrix.shape[1], columns, columns)
+    ends = [sum(ranks[: count + 1]) for count in range(len(ranks))]
+    recept, decay_sum, keyed, value, icl_sum = jnp.split(mixed, ends, axis=1)
+    decay_low = jnp.tanh(decay_sum).astype(jnp.bfloat16)
+    icl_low = icl_sum.astype(jnp.bfloat16)
     decay_in = mine(fading_offset_entry) + dot(decay_low, mine(fading_right_matrix))
     icl_in = mine(learning_rate_offset) + dot(icl_low, mine(learning_right_matrix))
     params = jnp.stack(

time: 423 us -> 327 us (0.77); the launches traced: 416 us -> 326 us
  matrix products: 118 us -> 30.4 us
  other arithmetic: 2.77 us -> 16 us
  waiting for transfers between devices: 132 us -> 119 us
  Pallas kernels: 92.1 us -> 86.7 us
    dot_general x5 -> x3, matrix products: 118 us -> 30.4 us  [dot(): return jnp.dot(left, right, preferred_element_type=jnp.float32)]
    all_gather x1, waiting for transfers between devices: 31.5 us -> 21.6 us  [by_heads(): lax.all_gather(packed_inputs_slab, ('seq', 'head'), axis=0, tiled=True)]
    unnamed x0 -> x3, other arithmetic: none -> 5.78 us
    pallas_call x1, Pallas kernels: 92.1 us -> 86.7 us  [mixed_heads(): pl.pallas_call(mixing_kernel, grid=(columns // PAIR, block_count // unrol...]
    convert_element_type x0 -> x3, other arithmetic: none -> 4.82 us  [by_heads(): earlier_maps.append((wide * coefs).astype(jnp.bfloat16))]
  transfers between devices with their start and end apart: 4 -> 4, of which waited for: 4 -> 4; matrix products, arithmetic and copies ran while one was open for 4% -> 9% of each run, Pallas kernels for 0% -> 0%
where the time goes in v2:
time: 327 us; the launch traced here: 326 us
  waiting for transfers between devices  119 us (36%)
  Pallas kernels  86.7 us (27%)
  matrix products  30.4 us (9%)
  starting transfers between devices  23.7 us (7%)
  local copies, waits for them, and re-layouts  18.7 us (6%)
  blocking collectives  17.9 us (5%)
  other arithmetic  16 us (5%)
  between operations  13.5 us (4%)
    all_to_all x3, waiting for transfers between devices, by_heads(): lax.all_to_all(array, 'seq', 1, 0, tiled=True)  96.4 us
    pallas_call x1, Pallas kernels, mixed_heads(): pl.pallas_call(mixing_kernel, grid=(columns // PAIR, block_count // unrol...  86.7 us
    dot_general x3, matrix products, dot(): return jnp.dot(left, right, preferred_element_type=jnp.float32)  30.4 us
    all_to_all x3, starting transfers between devices, by_heads(): lax.all_to_all(array, 'seq', 1, 0, tiled=True)  23.7 us
    all_gather x1, waiting for transfers between devices, by_heads(): lax.all_gather(packed_inputs_slab, ('seq', 'head'), axis=0, tiled=True)  21.6 us
    all_to_all x1, blocking collectives, by_heads(): return lax.all_to_all(lines, 'seq', 0, 1, tiled=True)  17.9 us
    unnamed x18, local copies, waits for them, and re-layouts  7.39 us
  transfers between devices with their start and end apart: 4, of which 4 were waited for; matrix products, arithmetic and copies ran while one was open for 9% of the time, Pallas kernels for 0%

profile of v2, /device:TPU:0, one launch (start us, length us, event | category | flops | bytes accessed | tf_op | source)
XLA Modules:
  0.0 325.7 jit_solution(17286447963688684048)
XLA Ops:
  6.5 0.0 copy-start
  6.5 0.7 all-gather.2.cloned.1.call-update
  7.3 0.5 copy-done
  7.8 1.2 copy_bitcast_fusion.2
  9.0 7.4 %all-to-all-start = ((bf16[256,16,128]{2,0,1:T(8,128)(2,1)}), bf16[256,16,128]{2,0,1:T(8,128)(2,1)S(1)}, u32[]{:S(2)}, u32[]{:S(2)}) async-start(bf16[256,16,128]{2,0,1:T(8,128)(2,1)} %copy_bitcast_fusion.2), calls=%async_computation | async-start | bytes 2097152 | tf_op jit(solution)/shard_map/all_to_all | solution.py:488
  16.4 0.8 reduce-window.9
  17.2 0.7 bitcast_subtract_fusion
  17.9 0.1 fusion.23
  18.0 0.1 broadcast_in_dim.14
  18.1 0.1 reshape.107
  18.1 0.8 dynamic-slice_bitcast_fusion
  18.9 0.8 dynamic-slice_bitcast_fusion.2
  19.7 0.6 convert_subtract_fusion.keep_ref
  20.3 1.3 fusion.27
  21.7 1.3 copy_bitcast_fusion.1
  22.9 27.4 %all-to-all-done = bf16[256,16,128]{2,0,1:T(8,128)(2,1)S(1)} async-done(((bf16[256,16,128]{2,0,1:T(8,128)(2,1)}), bf16[256,16,128]{2,0,1:T(8,128)(2,1)S(1)}, u32[]{:S(2)}, u32[]{:S(2)}) %all-to-all-start) | async-done | bytes 1048608 | tf_op jit(solution)/shard_map/all_to_all | solution.py:488
  50.3 6.9 %all-to-all-start.1 = ((bf16[256,16,128]{2,0,1:T(8,128)(2,1)}), bf16[256,16,128]{2,0,1:T(8,128)(2,1)S(1)}, u32[]{:S(2)}, u32[]{:S(2)}) async-start(bf16[256,16,128]{2,0,1:T(8,128)(2,1)} %copy_bitcast_fusion.1), calls=%async_computation.1 | async-start | bytes 2097152 | tf_op jit(solution)/shard_map/all_to_all | solution.py:488
  57.2 0.6 pad_maximum_fusion.params_ref
  57.8 0.8 dynamic_slice.26
  58.6 0.8 dynamic_slice.24
  59.4 1.2 copy_bitcast_fusion
  60.6 1.2 fusion.9
  61.8 1.1 constant_dynamic-update-slice_fusion.5
  63.0 34.2 %all-to-all-done.1 = bf16[256,16,128]{2,0,1:T(8,128)(2,1)S(1)} async-done(((bf16[256,16,128]{2,0,1:T(8,128)(2,1)}), bf16[256,16,128]{2,0,1:T(8,128)(2,1)S(1)}, u32[]{:S(2)}, u32[]{:S(2)}) %all-to-all-start.1) | async-done | bytes 1048608 | tf_op jit(solution)/shard_map/all_to_all | solution.py:488
  97.2 9.4 %all-to-all-start.2 = ((bf16[256,16,128]{2,0,1:T(8,128)(2,1)}), bf16[256,16,128]{2,0,1:T(8,128)(2,1)}, u32[]{:S(2)}, u32[]{:S(2)}) async-start(bf16[256,16,128]{2,0,1:T(8,128)(2,1)} %copy_bitcast_fusion), calls=%async_computation.2 | async-start | bytes 2097152 | tf_op jit(solution)/shard_map/all_to_all | solution.py:488
  106.6 2.7 fusion.13
  109.3 1.2 fusion.7
  110.5 1.1 constant_dynamic-update-slice_fusion.4
  111.7 34.8 %all-to-all-done.2 = bf16[256,16,128]{2,0,1:T(8,128)(2,1)} async-done(((bf16[256,16,128]{2,0,1:T(8,128)(2,1)}), bf16[256,16,128]{2,0,1:T(8,128)(2,1)}, u32[]{:S(2)}, u32[]{:S(2)}) %all-to-all-start.2) | async-done | bytes 1048608 | tf_op jit(solution)/shard_map/all_to_all | solution.py:488
  146.5 2.4 fusion.5
  148.9 1.2 constant_dynamic-update-slice_fusion.3
  150.1 1.5 fusion.11
  151.6 1.1 constant_dynamic-update-slice_fusion.2
  152.7 1.5 fusion.12
  154.3 1.1 constant_dynamic-update-slice_fusion.1
  155.4 1.1 constant_dynamic-update-slice_fusion
  156.6 1.5 fusion.10
  158.1 21.6 %all-gather.2.cloned.1.call-done = bf16[2048,4096]{1,0:T(8,128)(2,1)} async-done(((bf16[64,4096]{1,0:T(8,128)(2,1)}), bf16[2048,4096]{1,0:T(8,128)(2,1)}) %all-gather.2.cloned.1.call-update) | async-done | bytes 16777232 | tf_op jit(solution)/shard_map/all_gather | solution.py:486
  179.7 26.3 %convolution_bitcast_fusion = f32[2048,1280]{1,0:T(8,128)S(1)} fusion(bf16[2048,4096]{1,0:T(8,128)(2,1)} %all-gather.2.cloned.1.call-done, bf16[4096,1280]{1,0:T(8,128)(2,1)} %fusion.10), kind=kOutput, calls=%fused_computation | convolution fusion | flops 21474836480 | bytes 37748736 | tf_op jit(solution)/shard_map/dot_general | solution.py:499
  205.9 0.3 slice.29
  206.3 1.1 slice_add_fusion
  207.4 1.7 fusion.26
  209.2 2.1 convolution_add_fusion.icl_ref
  211.3 2.1 convolution_add_fusion.1.decay_ref
  213.4 86.7 %shard_map.154 = bf16[2048,128]{1,0:T(8,128)(2,1)} custom-call(f32[32]{0:T(128)} %convert_subtract_fusion.keep_ref, f32[2048,128]{1,0:T(8,128)} %get-tuple-element.7.recept_ref, f32[2048,128]{1,0:T(8,128)} %get-tuple-element.6.keyed_ref, f32[2048,128]{1,0:T(8,128)} %get-tuple-element.5.value_ref, f32[2048,128]{1,0:T(8,128)} %convolution_add_fusion.1.decay_ref, ...), custom_call_target="tpu_custom_call" | custom-call | tf_op jit(solution)/shard_map/pallas_call | solution.py:449
  300.1 17.9 %all_to_all.58 = bf16[16,128,128]{2,1,0:T(8,128)(2,1)S(1)} all-to-all(bf16[16,128,128]{2,1,0:T(8,128)(2,1)} %bitcast.69), channel_id=1, replica_groups=mesh['seq'=16,'head'=2] {'seq'}, dimensions={0} | all-to-all | bytes 1048576 | tf_op jit(solution)/shard_map/all_to_all | solution.py:532
  318.0 0.9 copy_bitcast_fusion.3
  318.9 0.0 copy-done.1
  (16 shorter events, 0.0 us)
Async XLA Ops:
  6.5 1.2 copy-start
  6.5 15.1 %copy-start.4 = (bf16[256,2048]{1,0:T(8,128)(2,1)S(1)}, bf16[256,2048]{1,0:T(8,128)(2,1)}, u32[]{:S(2)}) copy-start(bf16[256,2048]{1,0:T(8,128)(2,1)} %param.19) | copy-start | bytes 3145732
  6.5 52.8 %copy-start.5 = (bf16[256,2048]{1,0:T(8,128)(2,1)S(1)}, bf16[256,2048]{1,0:T(8,128)(2,1)}, u32[]{:S(2)}) copy-start(bf16[256,2048]{1,0:T(8,128)(2,1)} %param.20) | copy-start | bytes 3145732
  6.5 173.1 %all-gather.2.cloned.1.call-start = ((), (), s32[]{:S(2)}) async-start(), calls=%async_computation.4 | async-start | bytes 17301504 | tf_op jit(solution)/shard_map/all_gather | solution.py:486
  9.0 41.3 %all-to-all-start = ((bf16[256,16,128]{2,0,1:T(8,128)(2,1)}), bf16[256,16,128]{2,0,1:T(8,128)(2,1)S(1)}, u32[]{:S(2)}, u32[]{:S(2)}) async-start(bf16[256,16,128]{2,0,1:T(8,128)(2,1)} %copy_bitcast_fusion.2), calls=%async_computation | async-start | bytes 2097152 | tf_op jit(solution)/shard_map/all_to_all | solution.py:488
  50.3 46.8 %all-to-all-start.1 = ((bf16[256,16,128]{2,0,1:T(8,128)(2,1)}), bf16[256,16,128]{2,0,1:T(8,128)(2,1)S(1)}, u32[]{:S(2)}, u32[]{:S(2)}) async-start(bf16[256,16,128]{2,0,1:T(8,128)(2,1)} %copy_bitcast_fusion.1), calls=%async_computation.1 | async-start | bytes 2097152 | tf_op jit(solution)/shard_map/all_to_all | solution.py:488
  97.2 49.3 %all-to-all-start.2 = ((bf16[256,16,128]{2,0,1:T(8,128)(2,1)}), bf16[256,16,128]{2,0,1:T(8,128)(2,1)}, u32[]{:S(2)}, u32[]{:S(2)}) async-start(bf16[256,16,128]{2,0,1:T(8,128)(2,1)} %copy_bitcast_fusion), calls=%async_computation.2 | async-start | bytes 2097152 | tf_op jit(solution)/shard_map/all_to_all | solution.py:488
  111.7 41.1 %copy-start.2 = (bf16[4096,128]{1,0:T(8,128)(2,1)S(1)}, bf16[4096,128]{1,0:T(8,128)(2,1)}, u32[]{:S(2)}) copy-start(bf16[4096,128]{1,0:T(8,128)(2,1)} %param.22) | copy-start | bytes 3145732
  146.5 3.6 %copy-start.3 = (bf16[4096,128]{1,0:T(8,128)(2,1)S(1)}, bf16[4096,128]{1,0:T(8,128)(2,1)}, u32[]{:S(2)}) copy-start(bf16[4096,128]{1,0:T(8,128)(2,1)} %param.25) | copy-start | bytes 3145732
  209.2 109.7 %copy-start.1 = (bf16[256,2048]{1,0:T(8,128)(2,1)S(1)}, bf16[256,2048]{1,0:T(8,128)(2,1)}, u32[]{:S(2)}) copy-start(bf16[256,2048]{1,0:T(8,128)(2,1)} %param.18) | copy-start | bytes 3145732
Sparse Core Ops, SparseCore 0:
  10.2 169.3 all-gather.1

commit v3 on v1

--- a/solution.py
+++ b/solution.py
@@ -296,6 +296,12 @@
     return contract(left, right, 1, 0)
 
 
+def mm_once(left, right):
+    return jnp.dot(
+        left.astype(jnp.bfloat16), right.astype(jnp.bfloat16), preferred_element_type=jnp.float32
+    )
+
+
 def mm_nt(left, right):
     return contract(left, right, 1, 1)
 
@@ -368,58 +374,88 @@
     alpha = -unit_key
     bonus = head_sum(recept * key_mod * reward) * value
 
-    terms = []
-    for index in range(recept.shape[0] // SPAN):
-        rows = slice(index * SPAN, (index + 1) * SPAN)
-        decay_b = log_decay[rows]
-        log_sums = running_sum(decay_b)
-        decay_in = jnp.exp(log_sums)
-        inverse = jnp.exp(-log_sums)
-        decay_out = jnp.exp(log_sums[SPAN - 1 :] - log_sums)
-        alpha_s = stack(alpha[rows] * jnp.exp(log_sums - decay_b))
-        recept_s = stack(recept[rows] * decay_in)
-        left = jnp.concatenate([alpha_s, recept_s], axis=0)
-        right = jnp.concatenate(
-            [stack(beta[rows] * inverse), stack(key_mod[rows] * inverse)], axis=0
-        )
-        scores = mm_nt(split(left), split(right))
-        within = jnp.where(strict, scores[:PAIR, :PAIR], 0.0)
-        key_read = jnp.where(strict, scores[:PAIR, PAIR:], 0.0)
-        out_beta = jnp.where(on_or_below, scores[PAIR:, :PAIR], 0.0)
-        out_key = jnp.where(on_or_below, scores[PAIR:, PAIR:], 0.0)
-        value_s = split(stack(value[rows]))
-        from_value = mm(split(jnp.concatenate([key_read, out_key], axis=0)), value_s)
-        solver = eye
-        size = 1
-        while size < SPAN:
-            pair_mask = jnp.logical_and(
-                row // (2 * size) == col // (2 * size), row // size != col // size
-            )
-            corner = jnp.where(pair_mask, within, 0.0)
-            if size == 1:
-                solver = solver + corner
-            else:
-                halves = split(solver)
-                solver = solver + mm(halves, split(mm(split(corner), halves)))
-            size *= 2
-        right_side = jnp.concatenate([alpha_s, from_value[:PAIR]], axis=1)
-        reads = mm(split(solver), split(right_side))
-        reads_split = split(reads)
-        seen = mm(split(out_beta), reads_split)
-        queries = recept_s + seen[:, :PAIR]
-        base = seen[:, PAIR:] + from_value[PAIR:]
-        beta_out = split(stack(beta[rows] * decay_out))
-        key_out = split(stack(key_mod[rows] * decay_out))
-        moved = mm_tn(reads_split, beta_out)
-        step_map = jnp.where(row == col, decay_in[SPAN - 1 :], 0.0) + moved[:PAIR]
-        step_add = moved[PAIR:] + mm_tn(value_s, key_out)
-        terms.append((split(queries), base, split(step_map), step_add))
+    group = [slice(at, at + SPAN) for at in range(0, recept.shape[0], SPAN)]
+
+    def each(function, *lists):
+        return [function(*items) for items in zip(*lists)]
+
+    decays = [log_decay[rows] for rows in group]
+    sums = each(running_sum, decays)
+    decay_ins = each(jnp.exp, sums)
+    inverses = each(lambda total: jnp.exp(-total), sums)
+    decay_outs = each(lambda total: jnp.exp(total[SPAN - 1 :] - total), sums)
+    alphas = each(
+        lambda rows, total, decay: stack(alpha[rows] * jnp.exp(total - decay)), group, sums, decays
+    )
+    recepts = each(lambda rows, decay: stack(recept[rows] * decay), group, decay_ins)
+    lefts = each(lambda one, two: split(jnp.concatenate([one, two], axis=0)), alphas, recepts)
+    rights = each(
+        lambda rows, inverse: split(
+            jnp.concatenate([stack(beta[rows] * inverse), stack(key_mod[rows] * inverse)], axis=0)
+        ),
+        group,
+        inverses,
+    )
+    scores = each(mm_nt, lefts, rights)
+    withins = [jnp.where(strict, score[:PAIR, :PAIR], 0.0) for score in scores]
+    out_betas = [jnp.where(on_or_below, score[PAIR:, :PAIR], 0.0) for score in scores]
+    reads_and_outs = [
+        jnp.concatenate(
+            [
+                jnp.where(strict, score[:PAIR, PAIR:], 0.0),
+                jnp.where(on_or_below, score[PAIR:, PAIR:], 0.0),
+            ],
+            axis=0,
+        )
+        for score in scores
+    ]
+    values = [split(stack(value[rows])) for rows in group]
+    from_values = each(lambda scored, pair: mm_once(scored, pair[0]), reads_and_outs, values)
+    solvers = None
+    size = 1
+    while size < SPAN:
+        pair_mask = jnp.logical_and(
+            row // (2 * size) == col // (2 * size), row // size != col // size
+        )
+        corners = [jnp.where(pair_mask, within, 0.0) for within in withins]
+        if size == 1:
+            solvers = [eye + corner for corner in corners]
+        else:
+            rounded = [solver.astype(jnp.bfloat16) for solver in solvers]
+            inner = each(mm_once, corners, rounded)
+            outer = each(mm_once, rounded, inner)
+            solvers = each(jnp.add, solvers, outer)
+        size *= 2
+    checks = each(lambda within, solver: mm(split(within), split(solver)), withins, solvers)
+    residuals = each(lambda solver, check: eye - solver + check, solvers, checks)
+    fixes = each(mm_once, solvers, residuals)
+    solvers = each(lambda solver, fix: split(solver + fix), solvers, fixes)
+    right_sides = each(
+        lambda one, two: split(jnp.concatenate([one, two[:PAIR]], axis=1)), alphas, from_values
+    )
+    reads = each(lambda solver, side: split(mm(solver, side)), solvers, right_sides)
+    seens = each(lambda out_beta, read: mm_once(out_beta, read[0]), out_betas, reads)
+    beta_outs = each(lambda rows, decay: split(stack(beta[rows] * decay)), group, decay_outs)
+    key_outs = each(lambda rows, decay: split(stack(key_mod[rows] * decay)), group, decay_outs)
+    moves = each(mm_tn, reads, beta_outs)
+    adds = each(mm_tn, values, key_outs)
+    terms = [
+        (
+            (recepts[at] + seens[at][:, :PAIR]).astype(jnp.bfloat16),
+            seens[at][:, PAIR:] + from_values[at][PAIR:],
+            split(jnp.where(row == col, decay_ins[at][SPAN - 1 :], 0.0) + moves[at][:PAIR]),
+            moves[at][PAIR:] + adds[at],
+        )
+        for at in range(len(group))
+    ]
 
     state = state_ref[...]
     results = []
     for index, (queries, base, step_map, step_add) in enumerate(terms):
         state = split(state * keep_ref[step * len(terms) + index])
-        result = base + mm_nt(queries, state)
+        result = base + lax.dot_general(
+            queries, state[0], (((1,), (1,)), ((), ())), preferred_element_type=jnp.float32
+        )
         results.append(result[:SPAN] + result[SPAN:])
         state = mm(state, step_map) + step_add
     state_ref[...] = state
@@ -446,6 +482,140 @@
         out_shape=jax.ShapeDtypeStruct((row_count, columns), jnp.bfloat16),
         scratch_shapes=[pltpu.VMEM((PAIR, PAIR), jnp.float32)],
     )(keep, recept, keyed, value, decay_in, icl_in, params)
+
+
+CHIP_CORES = 2
+SIDE = 2
+
+
+def exchange_kernel(lines, seq_count, features, first, second, third, whole, own, sems, arrivals, local):
+    place, up = lax.axis_index("seq"), lax.axis_index("head")
+    layers = seq_count // (SIDE * CHIP_CORES)
+    core = lax.rem(place, CHIP_CORES)
+    side = lax.rem(place // CHIP_CORES, SIDE)
+    far = place // (CHIP_CORES * SIDE)
+    other_core, other_side, other_up = 1 - core, 1 - side, 1 - up
+    mesh_ids = pl.DeviceIdType.MESH
+
+    def at(far_index, side_index, core_index):
+        return (far_index * SIDE + side_index) * CHIP_CORES + core_index
+
+    barrier = pltpu.get_barrier_semaphore()
+    side_place = at(far, other_side, core)
+    core_place = at(far, side, other_core)
+    peers = [lax.rem(place + step, seq_count) for step in range(1, seq_count)]
+    for peer in peers:
+        pl.semaphore_signal(barrier, inc=1, device_id=(peer, up), device_id_type=mesh_ids)
+    pl.semaphore_signal(barrier, inc=1, device_id=(place, other_up), device_id_type=mesh_ids)
+    pl.semaphore_wait(barrier, seq_count)
+
+    counter = [0]
+    started = []
+
+    def send(source, target, device):
+        slot = counter[0]
+        counter[0] += 1
+        copy = pltpu.make_async_remote_copy(
+            src_ref=source,
+            dst_ref=target,
+            send_sem=sems.at[slot],
+            recv_sem=arrivals.at[slot],
+            device_id=device,
+            device_id_type=mesh_ids,
+        )
+        copy.start()
+        started.append(copy)
+        return copy
+
+    def block(seq_index, head_index, start=0, count=lines):
+        row = (seq_index * 2 + head_index) * lines + start
+        return whole.at[pl.ds(pl.multiple_of(row, 16), count), :]
+
+    mine = block(place, up)
+    along = [None]
+    for step in range(1, layers):
+        along.append(send(features, mine, (at(lax.rem(far + step, layers), side, core), up)))
+    to_side, to_up = [], []
+    to_side.append(send(features, mine, (side_place, up)))
+    to_up.append(send(features, mine, (place, other_up)))
+    to_core = [send(features, mine, (core_place, up))]
+    kept = pltpu.make_async_copy(features, mine, local.at[0])
+    kept.start()
+
+    columns = own.shape[2]
+    depth = first.shape[0]
+    kept_maps, sent_maps = [], []
+    for index, matrix in enumerate((first, second, third)):
+        target = own.at[index, pl.ds(pl.multiple_of(place * depth, 16), depth), :]
+        for peer in peers:
+            source = matrix.at[:, pl.ds(pl.multiple_of(peer * columns, 128), columns)]
+            sent_maps.append(send(source, target, (peer, up)))
+        source = matrix.at[:, pl.ds(pl.multiple_of(place * columns, 128), columns)]
+        kept_maps.append(pltpu.make_async_copy(source, target, local.at[index + 1]))
+        kept_maps[-1].start()
+
+    origins = [far] + [lax.rem(far + layers - step, layers) for step in range(1, layers)]
+    for step in range(1, layers):
+        along[step].wait_recv()
+        got = block(at(origins[step], side, core), up)
+        to_side.append(send(got, got, (side_place, up)))
+        to_up.append(send(got, got, (place, other_up)))
+        to_core.append(send(got, got, (core_place, up)))
+    half = lines // 2
+    corners = []
+    for step in range(layers):
+        to_side[step].wait_recv()
+        source = at(origins[step], other_side, core)
+        part = block(source, up, 0, half)
+        corner_up = send(part, part, (place, other_up))
+        got = block(source, up)
+        to_core.append(send(got, got, (core_place, up)))
+        to_up[step].wait_recv()
+        source = at(origins[step], side, core)
+        part = block(source, other_up, half, half)
+        corner_side = send(part, part, (side_place, up))
+        got = block(source, other_up)
+        to_core.append(send(got, got, (core_place, up)))
+        corners.append((corner_up, corner_side))
+    for step in range(layers):
+        for copy in corners[step]:
+            copy.wait_recv()
+        got = block(at(origins[step], other_side, core), other_up)
+        to_core.append(send(got, got, (core_place, up)))
+    for copy in to_core:
+        copy.wait_recv()
+    for copy in sent_maps:
+        copy.wait_recv()
+    for copy in started:
+        copy.wait_send()
+    kept.wait()
+    for copy in kept_maps:
+        copy.wait()
+
+
+def exchange(features, matrices):
+    seq_count = lax.axis_size("seq")
+    lines, model = features.shape
+    depth, width = matrices[0].shape
+    columns = width // seq_count
+    layers = seq_count // (SIDE * CHIP_CORES)
+    copies = (layers - 1) + 8 * layers + 3 * (seq_count - 1)
+    anywhere = pl.BlockSpec(memory_space=pl.ANY)
+    return pl.pallas_call(
+        functools.partial(exchange_kernel, lines, seq_count),
+        in_specs=[anywhere] * 4,
+        out_specs=(anywhere, anywhere),
+        out_shape=(
+            jax.ShapeDtypeStruct((lines * seq_count * 2, model), features.dtype),
+            jax.ShapeDtypeStruct((3, depth * seq_count, columns), features.dtype),
+        ),
+        scratch_shapes=[
+            pltpu.SemaphoreType.DMA((copies,)),
+            pltpu.SemaphoreType.DMA((copies,)),
+            pltpu.SemaphoreType.DMA((4,)),
+        ],
+        compiler_params=pltpu.CompilerParams(collective_id=0, has_side_effects=True),
+    )(features, *matrices)
 
 
 def by_heads(
@@ -473,11 +643,14 @@
     def mine(array):
         return lax.dynamic_slice_in_dim(array, start, columns, axis=array.ndim - 1)
 
-    gathered = lax.all_gather(packed_inputs_slab, ("seq", "head"), axis=0, tiled=True)
-    own_recept, own_key, own_value = [
-        lax.all_to_all(array, "seq", 1, 0, tiled=True)
-        for array in (acceptor_projector, address_projector, payload_projector)
-    ]
+    matrices = (acceptor_projector, address_projector, payload_projector)
+    if lax.axis_size("head") == 2 and seq_count % (SIDE * CHIP_CORES) == 0:
+        gathered, (own_recept, own_key, own_value) = exchange(packed_inputs_slab, matrices)
+    else:
+        gathered = lax.all_gather(packed_inputs_slab, ("seq", "head"), axis=0, tiled=True)
+        own_recept, own_key, own_value = [
+            lax.all_to_all(array, "seq", 1, 0, tiled=True) for array in matrices
+        ]
     row_count = gathered.shape[0]
     block_count = row_count // SPAN
     doc_starts = jnp.cumsum(paper_spans_sizes) - paper_spans_sizes

time: 423 us -> 314 us (0.74)
  waiting for transfers between devices: 132 us -> 0 us
  Pallas kernels: 92.1 us -> 148 us
  starting transfers between devices: 23.7 us -> 0 us
  blocking collectives: 18 us -> 34 us
  between operations: 13.7 us -> 0.3 us
  local copies, waits for them, and re-layouts: 15.8 us -> 5.41 us
    pallas_call x0 -> x1, Pallas kernels: none -> 113 us  [exchange(): pl.pallas_call(functools.partial(exchange_kernel, lines, seq_count), in_s...]
    all_to_all x3 -> x0, waiting for transfers between devices: 99.9 us -> none  [by_heads(): lax.all_to_all(array, 'seq', 1, 0, tiled=True)]
    pallas_call x1, Pallas kernels: 92.1 us -> 34.8 us  [mixed_heads(): pl.pallas_call(mixing_kernel, grid=(columns // PAIR, block_count // unrol...]
    all_gather x1 -> x0, waiting for transfers between devices: 31.5 us -> none  [by_heads(): lax.all_gather(packed_inputs_slab, ('seq', 'head'), axis=0, tiled=True)]
    all_to_all x3 -> x0, starting transfers between devices: 23.7 us -> none  [by_heads(): lax.all_to_all(array, 'seq', 1, 0, tiled=True)]
    all_to_all x1, blocking collectives: 18 us -> 34 us  [by_heads(): return lax.all_to_all(lines, 'seq', 0, 1, tiled=True)]
    unnamed x7 -> x6, local copies, waits for them, and re-layouts: 6.82 us -> 0.01 us
  transfers between devices with their start and end apart: 4 -> 0, of which waited for: 4 -> 0; matrix products, arithmetic and copies ran while one was open for 4% -> 0% of each run, Pallas kernels for 0% -> 0%
where the time goes in v3:
time: 314 us; the launch traced here: 307 us
  Pallas kernels  148 us (47%)
  matrix products  117 us (37%)
  blocking collectives  34 us (11%)
  local copies, waits for them, and re-layouts  5.41 us (2%)
    dot_general x5, matrix products, dot(): return jnp.dot(left, right, preferred_element_type=jnp.float32)  117 us
    pallas_call x1, Pallas kernels, exchange(): pl.pallas_call(functools.partial(exchange_kernel, lines, seq_count), in_s...  113 us
    pallas_call x1, Pallas kernels, mixed_heads(): pl.pallas_call(mixing_kernel, grid=(columns // PAIR, block_count // unrol...  34.8 us
    all_to_all x1, blocking collectives, by_heads(): return lax.all_to_all(lines, 'seq', 0, 1, tiled=True)  34 us

profile of v3, /device:TPU:0, one launch (start us, length us, event | category | flops | bytes accessed | tf_op | source)
XLA Modules:
  0.0 307.4 jit_solution(10072214473277994649)
XLA Ops:
  0.0 0.0 copy-start
  0.0 0.9 reduce-window.9
  0.9 0.7 bitcast_subtract_fusion
  1.6 0.1 fusion.41
  1.7 0.5 convert_subtract_fusion.1.keep_ref
  2.2 1.3 fusion.44
  3.5 0.1 broadcast_in_dim.12
  3.5 0.1 reshape.52
  3.6 112.9 %shard_map.154 = (bf16[2048,4096]{1,0:T(8,128)(2,1)}, bf16[3,4096,128]{2,1,0:T(8,128)(2,1)}) custom-call(bf16[64,4096]{1,0:T(8,128)(2,1)} %features.1, bf16[256,2048]{1,0:T(8,128)(2,1)} %first.1, bf16[256,2048]{1,0:T(8,128)(2,1)} %second.1, bf16[256,2048]{1,0:T(8,128)(2,1)} %third.1), custom_call_target="tpu_custom_call" | custom-call | tf_op jit(solution)/shard_map/pallas_call | solution.py:604
  116.5 0.0 copy-start.1
  116.5 22.7 %fusion.13.recept_ref = f32[2048,128]{1,0:T(8,128)} fusion(bf16[2048,4096]{1,0:T(8,128)(2,1)} %get-tuple-element.7, f32[4096]{0:T(1024)S(1)} %bitcast.40, bf16[3,4096,128]{2,1,0:T(8,128)(2,1)} %get-tuple-element.8, bf16[2047,4096]{1,0:T(8,128)(2,1)} %bitcast.41, pred[2048]{0:T(1024)(128)(4,1)S(1)} %fusion.40), kind=kOutput, calls=%fused_computation.16 | convolution fusion | flops 2206203904 | bytes 35670016 | tf_op jit(solution)/shard_map/dot_general | solution.py:665
  139.2 0.0 copy-done.1
  139.2 23.2 %fusion.11.keyed_ref = f32[2048,128]{1,0:T(8,128)} fusion(bf16[2048,4096]{1,0:T(8,128)(2,1)} %get-tuple-element.7, f32[4096]{0:T(1024)S(1)} %bitcast.39, bf16[3,4096,128]{2,1,0:T(8,128)(2,1)S(1)} %copy-done.1, bf16[2047,4096]{1,0:T(8,128)(2,1)} %bitcast.42, pred[2048]{0:T(1024)(128)(4,1)S(1)} %fusion.40), kind=kOutput, calls=%fused_computation.15 | convolution fusion | flops 2206203904 | bytes 35661824 | tf_op jit(solution)/shard_map/dot_general | solution.py:665
  162.4 22.8 %fusion.9.value_ref = f32[2048,128]{1,0:T(8,128)} fusion(bf16[2048,4096]{1,0:T(8,128)(2,1)} %get-tuple-element.7, f32[4096]{0:T(1024)S(1)} %bitcast.38, bf16[3,4096,128]{2,1,0:T(8,128)(2,1)S(1)} %copy-done.1, bf16[2047,4096]{1,0:T(8,128)(2,1)} %bitcast.43, pred[2048]{0:T(1024)(128)(4,1)S(1)} %fusion.40), kind=kOutput, calls=%fused_computation.14 | convolution fusion | flops 2206203904 | bytes 35661824 | tf_op jit(solution)/shard_map/dot_general | solution.py:665
  185.2 0.8 dynamic_slice.24
  185.9 0.8 dynamic_slice.26
  186.7 0.8 dynamic-slice_bitcast_fusion
  187.5 0.8 dynamic-slice_bitcast_fusion.2
  188.3 0.0 copy-done
  188.3 0.0 copy-start.2
  188.3 24.3 %convolution_add_fusion.1.decay_ref = f32[2048,128]{1,0:T(8,128)} fusion(bf16[4096,128]{1,0:T(8,128)(2,1)S(1)} %copy-done, bf16[2048,4096]{1,0:T(8,128)(2,1)} %get-tuple-element.7, f32[4096]{0:T(1024)S(1)} %bitcast.37, f32[128]{0:T(128)S(1)} %dynamic_slice.24, bf16[128,2048]{1,0:T(8,128)(2,1)} %param.23, s32[]{:T(128)S(6)} %select_n.27, ...), kind=kOutput, calls=%fused_computation.18 | convolution fusion | flops 2273837056 | bytes 35703300 | tf_op jit(solution)/shard_map/dot_general | solution.py:665
  212.6 0.0 copy-done.2
  212.6 24.3 %convolution_add_fusion.icl_ref = f32[2048,128]{1,0:T(8,128)} fusion(bf16[4096,128]{1,0:T(8,128)(2,1)S(1)} %copy-done.2, bf16[2048,4096]{1,0:T(8,128)(2,1)} %get-tuple-element.7, f32[4096]{0:T(1024)S(1)} %bitcast.36, f32[128]{0:T(128)S(1)} %dynamic_slice.26, bf16[128,2048]{1,0:T(8,128)(2,1)} %param.26, s32[]{:T(128)S(6)} %select_n.27, ...), kind=kOutput, calls=%fused_computation.17 | convolution fusion | flops 2273837056 | bytes 35703300 | tf_op jit(solution)/shard_map/dot_general | solution.py:665
  236.9 0.6 pad_maximum_fusion.params_ref
  237.5 34.8 %shard_map.155 = bf16[2048,128]{1,0:T(8,128)(2,1)} custom-call(f32[32]{0:T(128)} %convert_subtract_fusion.1.keep_ref, f32[2048,128]{1,0:T(8,128)} %fusion.13.recept_ref, f32[2048,128]{1,0:T(8,128)} %fusion.11.keyed_ref, f32[2048,128]{1,0:T(8,128)} %fusion.9.value_ref, f32[2048,128]{1,0:T(8,128)} %convolution_add_fusion.1.decay_ref, ...), custom_call_target="tpu_custom_call" | custom-call | tf_op jit(solution)/shard_map/pallas_call | solution.py:475
  272.2 34.0 %all_to_all.19 = bf16[16,128,128]{2,1,0:T(8,128)(2,1)S(1)} all-to-all(bf16[16,128,128]{2,1,0:T(8,128)(2,1)} %bitcast.35), channel_id=1, replica_groups=mesh['seq'=16,'head'=2] {'seq'}, dimensions={0} | all-to-all | bytes 1048576 | tf_op jit(solution)/shard_map/all_to_all | solution.py:687
  306.3 0.9 copy_bitcast_fusion
  (1 shorter events, 0.0 us)
Async XLA Ops:
  0.0 188.3 %copy-start = (bf16[4096,128]{1,0:T(8,128)(2,1)S(1)}, bf16[4096,128]{1,0:T(8,128)(2,1)}, u32[]{:S(2)}) copy-start(bf16[4096,128]{1,0:T(8,128)(2,1)} %param.22) | copy-start | bytes 3145732
  116.5 22.7 %copy-start.1 = (bf16[3,4096,128]{2,1,0:T(8,128)(2,1)S(1)}, bf16[3,4096,128]{2,1,0:T(8,128)(2,1)}, u32[]{:S(2)}) copy-start(bf16[3,4096,128]{2,1,0:T(8,128)(2,1)} %get-tuple-element.8) | copy-start | bytes 9437188
  188.3 24.3 %copy-start.2 = (bf16[4096,128]{1,0:T(8,128)(2,1)S(1)}, bf16[4096,128]{1,0:T(8,128)(2,1)}, u32[]{:S(2)}) copy-start(bf16[4096,128]{1,0:T(8,128)(2,1)} %param.25) | copy-start | bytes 3145732
